TPU v7x, 128 devices: a whole 4x4x4 slice. The times are simulated.
128 devices in a mesh: slab: 8 (over z, x_lo), view: 16 (over y, x_hi, core).
Axes of the slice: x: 4 (x_hi: 2, x_lo: 2; x = x_hi * 2 + x_lo), y: 4, z: 4, core: 2. Of those that a mesh axis runs over, the one named last changes fastest.
Arguments:
- volume: float32 [128, 32768], P(None, 'slab'), may hold values from 0 to 1
- measured: bfloat16 [32, 128, 2048], P('view'), may hold values from 0 to 8
- weights: bfloat16 [32, 32768, 1024], P('view', 'slab'), as said below
- offsets: int32 [32, 8], P('view', 'slab'), may hold values from 0 to 1024
- order: int32 [32], P('view'), may hold values from 0 to 1, as said below
Outputs:
- updated: float32 [128, 32768], P(None, 'slab')
- mismatch: float32 [32, 128, 2048], P('view')
Inputs may be any that keep to these rules, and one draw needn't show every extreme that they name: `order`: each aligned group of 2 entries is a permutation of 0 to 1. `weights`: every weight is zero or positive, and every voxel has a positive weight in every view.
All inputs are finite; a program needn't handle non-finite values.
Results may differ from a plain program's by a relative error of at most 0.00055.
Values sent between devices are 32-bit elements; how exact they have to be, the bound alone decides.
A program may use at most 128 MiB of HBM per device.

v0:
```python
import jax
import jax.numpy as jnp
from jax import lax
from jax.sharding import PartitionSpec as P

RELAXATION = 0.9


def in_blocks(array, dim, length):
    before, after = (array.shape[:dim], array.shape[dim + 1 :])
    return jnp.moveaxis(array.reshape(*before, length, -1, *after), dim, 0)


def sent_and_summed(array, axis, dim):
    tiles = in_blocks(array, dim, lax.axis_size(axis))
    arrived = lax.all_to_all(tiles, axis, split_axis=0, concat_axis=0, tiled=True)
    return arrived.sum(axis=0)


def sent_to_all(array, axis):
    length = lax.axis_size(axis)
    return lax.all_to_all(
        jnp.broadcast_to(array[None], (length, *array.shape)), axis, 0, 0, tiled=True
    )


def joined_along(tiles, dim):
    tiles = jnp.moveaxis(tiles, 0, dim)
    lengths = tiles.shape
    return tiles.reshape(*lengths[:dim], lengths[dim] * lengths[dim + 1], *lengths[dim + 2 :])


def collect(array, axis, dim):
    tiles = sent_to_all(array, axis)
    return joined_along(tiles, dim)


def per_device(volume, measured, weights, offsets, order):
    subsets = weights.shape[0]
    band_width = weights.shape[2]
    slice_rows = measured.shape[1]
    detector_cols = measured.shape[2]
    mismatch = jnp.zeros(measured.shape, jnp.float32)
    for subset_index in range(subsets):
        chosen_view = order[subset_index]
        footprint = lax.dynamic_index_in_dim(weights, chosen_view, 0, keepdims=False)
        first_column = offsets[chosen_view, 0]
        observed = lax.dynamic_index_in_dim(measured, chosen_view, 0, keepdims=False).astype(
            jnp.float32
        )
        partial_value = jnp.dot(
            volume.astype(jnp.bfloat16), footprint, preferred_element_type=jnp.float32
        )
        placed = lax.dynamic_update_slice(
            jnp.zeros((slice_rows, detector_cols), jnp.float32),
            partial_value,
            (jnp.int32(0), first_column),
        )
        placed_row = lax.dynamic_update_slice(
            jnp.zeros((detector_cols,), jnp.float32),
            jnp.sum(footprint, axis=0, dtype=jnp.float32),
            (first_column,),
        )
        projection_part, row_part = (
            sent_and_summed(placed, "slab", 1),
            sent_and_summed(placed_row, "slab", 0),
        )
        share_width = projection_part.shape[1]
        observed_part = lax.dynamic_slice_in_dim(
            observed, lax.axis_index("slab") * share_width, share_width, 1
        )
        correction_part = (observed_part - projection_part) / jnp.maximum(row_part, 1.0)
        correction = collect(correction_part, "slab", 1)
        mismatch = lax.dynamic_update_index_in_dim(mismatch, correction, chosen_view, 0)
        band_values = lax.dynamic_slice_in_dim(correction, first_column, band_width, 1).astype(
            jnp.bfloat16
        )
        back_terms = lax.dot_general(
            band_values, footprint, (((1,), (1,)), ((), ())), preferred_element_type=jnp.float32
        )
        col_total = jnp.sum(footprint, axis=1, dtype=jnp.float32)
        back_part, weight_part = (
            sent_and_summed(back_terms, "view", 1),
            sent_and_summed(col_total, "view", 0),
        )
        share_width = back_part.shape[1]
        volume_part = lax.dynamic_slice_in_dim(
            volume, lax.axis_index("view") * share_width, share_width, 1
        )
        new_part = volume_part + RELAXATION * back_part / weight_part[None, :]
        volume = lax.all_gather(new_part, "view", axis=1, tiled=True)
    return (volume, mismatch)


def solution(mesh):
    placed = (
        P(None, "slab"),
        P("view", None, None),
        P("view", "slab", None),
        P("view", "slab"),
        P("view"),
    )
    return jax.shard_map(
        per_device,
        mesh=mesh,
        in_specs=placed,
        out_specs=(P(None, "slab"), P("view", None, None)),
        check_vma=False,
    )
```

profile of v0, /device:TPU:1, one launch (start us, length us, event | category | flops | bytes accessed | tf_op | source)
XLA Modules:
  0.0 339.2 jit_solution(11723134778477959800)
XLA Ops:
  7.2 1.3 fusion.17
  12.4 1.4 constant_dynamic-slice_fusion
  15.0 13.8 %convert_reduce_fusion.2 = (f32[4096]{0:T(1024)}, f32[1024]{0:T(1024)S(1)}, bf16[1,4096,1024]{2,1,0:T(8,128)(2,1)}, f32[1024]{0:T(1024)S(1)}, f32[4096]{0:T(1024)}, /*index=5*/bf16[1,4096,1024]{2,1,0:T(8,128)(2,1)}) fusion(bf16[2,4096,1024]{2,1,0:T(8,128)(2,1)} %param.7, s32[]{:T(128)S(6)} %select_n.34, s32[]{:T(128)S(6)} %select_n.37), kind=kLoop, calls=%fused_computation.2 | loop fusion | flops 25155584 | bytes 33595400 | tf_op jit(solution)/shard_map/reduce_sum | solution.py:81
  29.4 0.6 broadcast.25.clone
  30.0 1.4 dynamic_update_slice.20
  31.5 6.8 %all-to-all-start.1 = ((f32[8,1,256]{2,1,0:T(1,128)}), f32[8,1,256]{2,1,0:T(1,128)S(1)}, u32[]{:S(2)}, u32[]{:S(2)}) async-start(f32[8,1,256]{2,1,0:T(1,128)} %bitcast.7), calls=%async_computation.1 | async-start | bytes 16384 | tf_op jit(solution)/shard_map/all_to_all | solution.py:16
  38.3 5.7 %fusion.4 = f32[128,1024]{0,1:T(8,128)S(1)} fusion(bf16[1,4096,1024]{2,1,0:T(8,128)(2,1)} %get-tuple-element.7, f32[128,4096]{1,0:T(8,128)S(1)} %copy-done), kind=kOutput, calls=%fused_computation.10 | convolution fusion | flops 1074266112 | bytes 11010048 | tf_op jit(solution)/shard_map/dot_general | solution.py:51
  44.0 1.0 broadcast.24.clone
  45.1 3.0 dynamic_update_slice.19
  48.0 5.1 %all-to-all-start = ((f32[8,128,256]{1,2,0:T(8,128)}), f32[8,128,256]{1,2,0:T(8,128)S(1)}, u32[]{:S(2)}, u32[]{:S(2)}) async-start(f32[8,128,256]{1,2,0:T(8,128)} %bitcast.6), calls=%async_computation | async-start | bytes 2097152 | tf_op jit(solution)/shard_map/all_to_all | solution.py:16
  53.2 0.9 dynamic-slice_convert_fusion.2
  54.2 13.2 %all-to-all-done = f32[8,128,256]{1,2,0:T(8,128)S(1)} async-done(((f32[8,128,256]{1,2,0:T(8,128)}), f32[8,128,256]{1,2,0:T(8,128)S(1)}, u32[]{:S(2)}, u32[]{:S(2)}) %all-to-all-start) | async-done | bytes 1048608 | tf_op jit(solution)/shard_map/all_to_all | solution.py:16
  67.4 0.1 fusion.14
  67.6 0.1 copy.39
  67.7 18.9 %all_to_all.66 = f32[8,128,256]{2,1,0:T(8,128)S(1)} all-to-all(f32[8,128,256]{2,1,0:T(8,128)S(1)} %broadcast_in_dim.13), channel_id=1, replica_groups=mesh['slab'=8,'view'=16] {'slab'}, dimensions={0} | all-to-all | bytes 2097152 | tf_op jit(solution)/shard_map/all_to_all | solution.py:22
  86.7 8.5 %all-to-all-start.4 = ((f32[16,1,256]{2,1,0:T(1,128)}), f32[16,1,256]{2,1,0:T(1,128)S(1)}, u32[]{:S(2)}, u32[]{:S(2)}) async-start(f32[16,1,256]{2,1,0:T(1,128)} %bitcast.13), calls=%async_computation.4 | async-start | bytes 32768 | tf_op jit(solution)/shard_map/all_to_all | solution.py:16
  95.3 7.6 %convolution_bitcast_fusion.1 = f32[16,128,256]{2,1,0:T(8,128)} fusion(bf16[16,256,1024]{2,1,0:T(8,128)(2,1)} %bitcast.63, bf16[128,2048]{1,0:T(8,128)(2,1)S(1)} %bitcast.68, s32[]{:T(128)S(6)} %select_n.36), kind=kOutput, calls=%fused_computation.9 | convolution fusion | flops 1073741824 | bytes 10747908 | tf_op jit(solution)/shard_map/dot_general | solution.py:78
  102.9 7.2 %all-to-all-start.3 = ((f32[16,128,256]{2,1,0:T(8,128)}), f32[16,128,256]{2,1,0:T(8,128)S(1)}, u32[]{:S(2)}, u32[]{:S(2)}) async-start(f32[16,128,256]{2,1,0:T(8,128)} %convolution_bitcast_fusion.1), calls=%async_computation.3 | async-start | bytes 4194304 | tf_op jit(solution)/shard_map/all_to_all | solution.py:16
  110.2 28.4 %all-to-all-done.3 = f32[16,128,256]{2,1,0:T(8,128)S(1)} async-done(((f32[16,128,256]{2,1,0:T(8,128)}), f32[16,128,256]{2,1,0:T(8,128)S(1)}, u32[]{:S(2)}, u32[]{:S(2)}) %all-to-all-start.3) | async-done | bytes 2097184 | tf_op jit(solution)/shard_map/all_to_all | solution.py:16
  138.6 0.1 reduce_sum.111
  138.7 1.6 divide_add_fusion.1
  142.1 0.6 broadcast.25.clone.1
  142.7 1.4 dynamic_update_slice.22
  144.2 3.3 all-to-all-start.6
  147.5 36.2 %all-gather.3.cloned.1.call-done = f32[128,4096]{1,0:T(8,128)} async-done(((f32[128,256]{1,0:T(8,128)}), f32[128,4096]{1,0:T(8,128)}) %all-gather.3.cloned.1.call-update) | async-done | bytes 2097168 | tf_op jit(solution)/shard_map/all_gather | solution.py:91
  183.7 7.4 %fusion = f32[128,1024]{0,1:T(8,128)S(1)} fusion(bf16[1,4096,1024]{2,1,0:T(8,128)(2,1)} %get-tuple-element.10, f32[128,4096]{1,0:T(8,128)} %all-gather.3.cloned.1.call-done), kind=kOutput, calls=%fused_computation.4 | convolution fusion | flops 1074266112 | bytes 11010048 | tf_op jit(solution)/shard_map/dot_general | solution.py:51
  191.1 1.0 broadcast.24
  192.1 3.0 dynamic_update_slice.21
  195.1 4.1 %all-to-all-start.5 = ((f32[8,128,256]{1,2,0:T(8,128)}), f32[8,128,256]{1,2,0:T(8,128)S(1)}, u32[]{:S(2)}, u32[]{:S(2)}) async-start(f32[8,128,256]{1,2,0:T(8,128)} %bitcast.19), calls=%async_computation.5 | async-start | bytes 2097152 | tf_op jit(solution)/shard_map/all_to_all | solution.py:16
  199.3 15.1 %all-to-all-done.5 = f32[8,128,256]{1,2,0:T(8,128)S(1)} async-done(((f32[8,128,256]{1,2,0:T(8,128)}), f32[8,128,256]{1,2,0:T(8,128)S(1)}, u32[]{:S(2)}, u32[]{:S(2)}) %all-to-all-start.5) | async-done | bytes 1048608 | tf_op jit(solution)/shard_map/all_to_all | solution.py:16
  214.5 0.1 fusion.13
  214.6 0.1 copy.46
  214.8 18.2 %all_to_all.67 = f32[8,128,256]{2,1,0:T(8,128)S(1)} all-to-all(f32[8,128,256]{2,1,0:T(8,128)S(1)} %broadcast_in_dim.14), channel_id=1, replica_groups=mesh['slab'=8,'view'=16] {'slab'}, dimensions={0} | all-to-all | bytes 2097152 | tf_op jit(solution)/shard_map/all_to_all | solution.py:22
  233.0 6.1 %all-to-all-start.9 = ((f32[16,1,256]{2,1,0:T(1,128)}), f32[16,1,256]{2,1,0:T(1,128)S(1)}, u32[]{:S(2)}, u32[]{:S(2)}) async-start(f32[16,1,256]{2,1,0:T(1,128)} %bitcast.26), calls=%async_computation.9 | async-start | bytes 32768 | tf_op jit(solution)/shard_map/all_to_all | solution.py:16
  239.2 7.6 %convolution_bitcast_fusion = f32[16,128,256]{2,1,0:T(8,128)} fusion(bf16[16,256,1024]{2,1,0:T(8,128)(2,1)} %bitcast.62, bf16[128,2048]{1,0:T(8,128)(2,1)S(1)} %bitcast.69, s32[]{:T(128)S(6)} %select_n.38), kind=kOutput, calls=%fused_computation.8 | convolution fusion | flops 1073741824 | bytes 10747908 | tf_op jit(solution)/shard_map/dot_general | solution.py:78
  246.7 7.2 %all-to-all-start.8 = ((f32[16,128,256]{2,1,0:T(8,128)}), f32[16,128,256]{2,1,0:T(8,128)}, u32[]{:S(2)}, u32[]{:S(2)}) async-start(f32[16,128,256]{2,1,0:T(8,128)} %convolution_bitcast_fusion), calls=%async_computation.8 | async-start | bytes 4194304 | tf_op jit(solution)/shard_map/all_to_all | solution.py:16
  254.1 28.5 %all-to-all-done.8 = f32[16,128,256]{2,1,0:T(8,128)} async-done(((f32[16,128,256]{2,1,0:T(8,128)}), f32[16,128,256]{2,1,0:T(8,128)}, u32[]{:S(2)}, u32[]{:S(2)}) %all-to-all-start.8) | async-done | bytes 2097184 | tf_op jit(solution)/shard_map/all_to_all | solution.py:16
  282.6 1.7 reduce_sum.117
  284.3 1.6 divide_add_fusion
  285.9 0.3 copy.40
  286.2 0.3 copy.50
  286.6 1.6 broadcast_in_dim.28
  288.1 1.1 constant_dynamic-update-slice_fusion
  289.2 0.3 copy.47
  289.5 0.3 copy.51
  289.9 1.1 constant_dynamic-update-slice_fusion.1
  291.0 38.3 %all-gather.5.cloned.1.call-done = f32[128,4096]{1,0:T(8,128)} async-done(((f32[128,256]{1,0:T(8,128)}), f32[128,4096]{1,0:T(8,128)}) %all-gather.5.cloned.1.call-update) | async-done | bytes 2097168 | tf_op jit(solution)/shard_map/all_gather | solution.py:91
  329.2 3.1 copy.76
  (24 shorter events, 0.8 us)
Async XLA Ops:
  15.0 23.3 %copy-start = (f32[128,4096]{1,0:T(8,128)S(1)}, f32[128,4096]{1,0:T(8,128)}, u32[]{:S(2)}) copy-start(f32[128,4096]{1,0:T(8,128)} %param.5) | copy-start | bytes 6291460
  31.5 16.5 %all-to-all-start.1 = ((f32[8,1,256]{2,1,0:T(1,128)}), f32[8,1,256]{2,1,0:T(1,128)S(1)}, u32[]{:S(2)}, u32[]{:S(2)}) async-start(f32[8,1,256]{2,1,0:T(1,128)} %bitcast.7), calls=%async_computation.1 | async-start | bytes 16384 | tf_op jit(solution)/shard_map/all_to_all | solution.py:16
  48.0 19.4 %all-to-all-start = ((f32[8,128,256]{1,2,0:T(8,128)}), f32[8,128,256]{1,2,0:T(8,128)S(1)}, u32[]{:S(2)}, u32[]{:S(2)}) async-start(f32[8,128,256]{1,2,0:T(8,128)} %bitcast.6), calls=%async_computation | async-start | bytes 2097152 | tf_op jit(solution)/shard_map/all_to_all | solution.py:16
  86.7 16.2 %all-to-all-start.4 = ((f32[16,1,256]{2,1,0:T(1,128)}), f32[16,1,256]{2,1,0:T(1,128)S(1)}, u32[]{:S(2)}, u32[]{:S(2)}) async-start(f32[16,1,256]{2,1,0:T(1,128)} %bitcast.13), calls=%async_computation.4 | async-start | bytes 32768 | tf_op jit(solution)/shard_map/all_to_all | solution.py:16
  102.9 35.7 %all-to-all-start.3 = ((f32[16,128,256]{2,1,0:T(8,128)}), f32[16,128,256]{2,1,0:T(8,128)S(1)}, u32[]{:S(2)}, u32[]{:S(2)}) async-start(f32[16,128,256]{2,1,0:T(8,128)} %convolution_bitcast_fusion.1), calls=%async_computation.3 | async-start | bytes 4194304 | tf_op jit(solution)/shard_map/all_to_all | solution.py:16
  110.1 73.6 %all-gather.3.cloned.1.call-start = ((), (), s32[]{:S(2)}) async-start(), calls=%async_computation.10 | async-start | bytes 2228224 | tf_op jit(solution)/shard_map/all_gather | solution.py:91
  144.2 50.9 %all-to-all-start.6 = ((f32[8,1,256]{2,1,0:T(1,128)}), f32[8,1,256]{2,1,0:T(1,128)S(1)}, u32[]{:S(2)}, u32[]{:S(2)}) async-start(f32[8,1,256]{2,1,0:T(1,128)} %bitcast.20), calls=%async_computation.6 | async-start | bytes 16384 | tf_op jit(solution)/shard_map/all_to_all | solution.py:16
  195.1 19.4 %all-to-all-start.5 = ((f32[8,128,256]{1,2,0:T(8,128)}), f32[8,128,256]{1,2,0:T(8,128)S(1)}, u32[]{:S(2)}, u32[]{:S(2)}) async-start(f32[8,128,256]{1,2,0:T(8,128)} %bitcast.19), calls=%async_computation.5 | async-start | bytes 2097152 | tf_op jit(solution)/shard_map/all_to_all | solution.py:16
  233.0 13.7 %all-to-all-start.9 = ((f32[16,1,256]{2,1,0:T(1,128)}), f32[16,1,256]{2,1,0:T(1,128)S(1)}, u32[]{:S(2)}, u32[]{:S(2)}) async-start(f32[16,1,256]{2,1,0:T(1,128)} %bitcast.26), calls=%async_computation.9 | async-start | bytes 32768 | tf_op jit(solution)/shard_map/all_to_all | solution.py:16
  246.7 35.8 %all-to-all-start.8 = ((f32[16,128,256]{2,1,0:T(8,128)}), f32[16,128,256]{2,1,0:T(8,128)}, u32[]{:S(2)}, u32[]{:S(2)}) async-start(f32[16,128,256]{2,1,0:T(8,128)} %convolution_bitcast_fusion), calls=%async_computation.8 | async-start | bytes 4194304 | tf_op jit(solution)/shard_map/all_to_all | solution.py:16
  254.0 75.2 %all-gather.5.cloned.1.call-start = ((), (), s32[]{:S(2)}) async-start(), calls=%async_computation.11 | async-start | bytes 2228224 | tf_op jit(solution)/shard_map/all_gather | solution.py:91
Sparse Core Ops, SparseCore 0:
  140.4 43.2 all-gather.2
  286.0 43.1 all-gather.4
where the time goes:
time: 340 us; the launch traced here: 339 us
  waiting for transfers between devices  160 us (47%)
  starting transfers between devices  48.5 us (14%)
  blocking collectives  37.1 us (11%)
  matrix products  28.3 us (8%)
  local copies, waits for them, and re-layouts  23.5 us (7%)
  between operations  21.9 us (6%)
  other arithmetic  20.2 us (6%)
    all_to_all x8, waiting for transfers between devices, sent_and_summed(): lax.all_to_all(tiles, axis, split_axis=0, concat_axis=0, tiled=True)  85.2 us
    all_gather x2, waiting for transfers between devices, per_device(): volume = lax.all_gather(new_part, 'view', axis=1, tiled=True)  74.4 us
    all_to_all x8, starting transfers between devices, sent_and_summed(): lax.all_to_all(tiles, axis, split_axis=0, concat_axis=0, tiled=True)  48.5 us
    all_to_all x2, blocking collectives, sent_to_all(): lax.all_to_all(jnp.broadcast_to(array[None], (length, *array.shape)), axi...  37.1 us
    dot_general x2, matrix products, per_device(): lax.dot_general(band_values, footprint, (((1,), (1,)), ((), ())), preferr...  15.2 us
    reduce_sum x1, other arithmetic, per_device(): col_total = jnp.sum(footprint, axis=1, dtype=jnp.float32)  13.8 us
    dot_general x2, matrix products, per_device(): jnp.dot(volume.astype(jnp.bfloat16), footprint, preferred_element_type=jn...  13.1 us
  transfers between devices with their start and end apart: 10, of which 6 were waited for; matrix products, arithmetic and copies ran while one was open for 13% of the time, Pallas kernels for 0%

commit v1 on v0

v1 whole, which is shorter than its diff:
```python
import jax
import jax.numpy as jnp
from jax import lax
from jax.experimental import pallas as pl
from jax.experimental.pallas import tpu as pltpu
from jax.sharding import PartitionSpec as P

RELAXATION = 0.9
MESH = pl.DeviceIdType.MESH
CHUNKS = 2
LANES = 128
KB = 512


def kernel(chunks, order_ref, off_ref, vol_hbm, meas_hbm, w_hbm, upd_hbm, mis_hbm,
           wv, vol, meas, acc, bandb, x1, xo, fs, fr, gs, gr, cor, rsum, csum,
           bk, rc, ry1, ry2, rx, local_sem, send_sem, recv_sem):
    slices, voxels = vol.shape
    rows = slices // chunks
    band = wv.shape[2]
    subsets = 2
    half = voxels // 2 // LANES
    nb = band // LANES

    s = lax.axis_index("slab")
    v = lax.axis_index("view")
    core = lax.rem(v, 2)
    xh = lax.rem(v // 2, 2)
    y = v // 4
    xl = lax.rem(s, 2)
    z = s // 2

    def slab_dev(other):
        return {"slab": other, "view": v}

    def view_dev(other):
        return {"slab": s, "view": other}

    y1 = y + 1 - 2 * lax.rem(y, 2)
    y3 = 3 - y
    y2 = lax.rem(y + 2, 4)
    dev_core = view_dev(v + 1 - 2 * core)
    dev_xh = view_dev(v + 2 - 4 * xh)
    dev_y1 = view_dev(v + 4 * (y1 - y))
    dev_y3 = view_dev(v + 4 * (y3 - y))
    s_mate = s + 1 - 2 * xl
    dev_mate = slab_dev(s_mate)
    dev_z = [None] + [slab_dev(lax.rem(z + k, 4) * 2 + xl) for k in (1, 2, 3)]

    used = [0]
    pending = []

    def remote(src, dst, dev, arrives=None):
        at = used[0]
        used[0] += 1
        cp = pltpu.make_async_remote_copy(
            src_ref=src, dst_ref=dst, send_sem=send_sem.at[at], recv_sem=recv_sem.at[at],
            device_id=dev, device_id_type=MESH)
        cp.start()
        pending.append(cp)
        if arrives is None:
            return cp
        return pltpu.make_async_remote_copy(
            src_ref=src, dst_ref=arrives, send_sem=send_sem.at[at], recv_sem=recv_sem.at[at],
            device_id=dev, device_id_type=MESH)

    steps = voxels // KB
    def w_copy(i):
        at = pl.ds(i * KB, KB)
        return pltpu.make_async_copy(w_hbm.at[:, at, :], wv.at[:, at, :], local_sem.at[i])
    vol_copies = []
    for c in range(chunks):
        at = pl.ds(c * rows, rows)
        cp = pltpu.make_async_copy(vol_hbm.at[at, :], vol.at[at, :], local_sem.at[steps + c])
        cp.start()
        vol_copies.append(cp)
        if c == 0:
            for i in range(steps):
                w_copy(i).start()
    meas_copies = []
    for hi in range(2):
        col = pl.multiple_of(hi * band + s * LANES, LANES)
        cp = pltpu.make_async_copy(meas_hbm.at[:, :, pl.ds(col, LANES)], meas.at[hi],
                                   local_sem.at[steps + chunks + hi])
        cp.start()
        meas_copies.append(cp)

    barrier = pltpu.get_barrier_semaphore()
    for k in range(1, 8):
        pl.semaphore_signal(barrier, inc=1, device_id=slab_dev(lax.rem(s + k, 8)), device_id_type=MESH)
    for dev in (dev_core, dev_xh, dev_y1, dev_y3):
        pl.semaphore_signal(barrier, inc=1, device_id=dev, device_id_type=MESH)
    pl.semaphore_wait(barrier, 11)

    column = lax.broadcasted_iota(jnp.int32, (8, LANES), 1) + s * LANES
    column = column.astype(jnp.float32)

    out_copies = []

    def chain(c):
        at_rows = pl.ds(c * rows, rows)
        ext = 8 if c == 0 else 0
        m = rows + 2 * ext
        r = rows + ext
        rr = pl.ds(0, r)
        only = pl.ds(0, rows)
        for t in range(subsets):
            view_t = order_ref[t]
            off = off_ref[view_t]
            shift = jnp.where(off >= band, 0, off)
            if t == 0:
                vol_copies[c].wait()
                if c == 0:
                    for i in range(steps):
                        w_copy(i).wait()
            acc[pl.ds(0, m), :] = jnp.zeros((m, band), jnp.float32)

            def forward(i, carry):
                if t == 0:
                    xk = vol[at_rows, pl.ds(pl.multiple_of(i * KB, KB), KB)]
                else:
                    xk = jnp.concatenate(
                        [x1[c, i * (KB // LANES) + j] for j in range(KB // LANES)], axis=1)
                xk = xk.astype(jnp.bfloat16)
                if ext:
                    xk = jnp.concatenate([xk, jnp.ones((2 * ext, KB), jnp.bfloat16)], axis=0)
                wk = wv[view_t, pl.ds(pl.multiple_of(i * KB, KB), KB), :]
                acc[pl.ds(0, m), :] += jnp.dot(xk, wk, preferred_element_type=jnp.float32)
                return carry

            lax.fori_loop(0, steps, forward, 0)
            folded = pltpu.roll(acc[rr, :], shift, 1)
            if ext:
                tail = folded[rows:, :]
                kind = lax.broadcasted_iota(jnp.int32, tail.shape, 0)
                tail = jnp.where(kind < 4, tail, off.astype(jnp.float32))
            for b in range(nb):
                fs[t, c, b, only, :] = folded[:rows, b * LANES:(b + 1) * LANES]
                if ext:
                    fs[t, c, b, pl.ds(rows, ext), :] = tail[:, b * LANES:(b + 1) * LANES]
            arrivals = []
            for k in range(1, 8):
                peer = lax.rem(s + k, 8)
                arrivals.append(remote(fs.at[t, c, peer, rr], fr.at[t, c, k, rr], slab_dev(peer)))
            yield
            fr[t, c, 0, rr, :] = fs[t, c, s, rr, :]
            for cp in arrivals:
                cp.wait_recv()
            if t == 0 and c == 0:
                for cp in meas_copies:
                    cp.wait()
            low = jnp.zeros((rows, LANES), jnp.float32)
            high = jnp.zeros((rows, LANES), jnp.float32)
            masks = []
            for k in range(8):
                offs = fr[t, 0, k, pl.ds(rows + 4, 1), :]
                masks.append(column[0:1, :] >= offs)
            if ext:
                rlow = jnp.zeros((1, LANES), jnp.float32)
                rhigh = jnp.zeros((1, LANES), jnp.float32)
                for k in range(8):
                    part = fr[t, c, k, pl.ds(rows, 1), :]
                    rlow += jnp.where(masks[k], part, 0.0)
                    rhigh += jnp.where(masks[k], 0.0, part)
                rsum[t, 0] = jnp.broadcast_to(jnp.maximum(rlow, 1.0), (8, LANES))
                rsum[t, 1] = jnp.broadcast_to(jnp.maximum(rhigh, 1.0), (8, LANES))
            for k in range(8):
                part = fr[t, c, k, only, :]
                low += jnp.where(masks[k], part, 0.0)
                high += jnp.where(masks[k], 0.0, part)
            seen_low = meas[0, view_t, at_rows, :].astype(jnp.float32)
            seen_high = meas[1, view_t, at_rows, :].astype(jnp.float32)
            low = (seen_low - low) / rsum[t, 0, pl.ds(0, 1), :]
            high = (seen_high - high) / rsum[t, 1, pl.ds(0, 1), :]
            cor[t, c, 0] = low
            cor[t, c, 1] = high
            arrivals = []
            for k in range(8):
                piece = jnp.where(masks[k], low, high)
                if k == 0:
                    gr[t, c, s] = piece
                else:
                    gs[t, c, k] = piece
                    arrivals.append(remote(
                        gs.at[t, c, k], gr.at[t, c, s], slab_dev(lax.rem(s + 8 - k, 8)),
                        gr.at[t, c, lax.rem(s + k, 8)]))
            own = pltpu.make_async_copy(cor.at[t, c], mis_hbm.at[t, c, s],
                                        local_sem.at[steps + chunks + 2 + t * chunks + c])
            own.start()
            out_copies.append(own)
            mate_in = remote(cor.at[t, c], mis_hbm.at[t, c, s], dev_mate, mis_hbm.at[t, c, s_mate])
            for k in (1, 2, 3):
                far = lax.rem(z + 4 - k, 4) * 2 + xl
                out_copies.append(("recv", remote(
                    cor.at[t, c], mis_hbm.at[t, c, s], dev_z[k], mis_hbm.at[t, c, far])))
            yield
            for cp in arrivals:
                cp.wait_recv()
            g = jnp.concatenate([gr[t, c, b] for b in range(nb)], axis=1)
            g = pltpu.roll(g, jnp.where(shift == 0, 0, band - shift), 1).astype(jnp.bfloat16)
            bandb[only, :] = g
            if ext:
                bandb[pl.ds(rows, 2 * ext), :] = jnp.ones((2 * ext, band), jnp.bfloat16)

            def backward(base):
                def step(n, carry):
                    vb = base + n * (KB // LANES)
                    wk = wv[view_t, pl.ds(pl.multiple_of(vb * LANES, LANES), KB), :]
                    res = lax.dot_general(bandb[pl.ds(0, m), :], wk, (((1,), (1,)), ((), ())),
                                          preferred_element_type=jnp.float32)
                    for j in range(KB // LANES):
                        bk[t, c, vb + j, rr, :] = res[:r, j * LANES:(j + 1) * LANES]
                    return carry
                lax.fori_loop(0, half * LANES // KB, step, 0)

            theirs = (1 - core) * half
            mine = core * half
            backward(theirs)
            core_in = remote(bk.at[t, c, pl.ds(theirs, half), rr], rc.at[t, c, :, rr], dev_core)
            backward(mine)
            mate_in.wait_recv()
            for k in (1, 2, 3):
                far = lax.rem(z + 4 - k, 4) * 2 + 1 - xl
                out_copies.append(("recv", remote(
                    mis_hbm.at[t, c, s_mate], mis_hbm.at[t, c, s_mate], dev_z[k],
                    mis_hbm.at[t, c, far])))
            yield
            core_in.wait_recv()

            def add(block, extra, start):
                for j in range(2):
                    at = mine + block + j
                    bk[t, c, at, rr, :] += rc[t, c, block + j, rr, :]
                    if extra is not None:
                        bk[t, c, at, rr, :] += extra[j, rr, :]

            ins = []
            for h in range(2):
                to, first = ((dev_y1, y1), (dev_y3, y3))[h]
                for j, yb in enumerate((first, y2)):
                    block = h * 8 + yb * 2
                    add(block, None, None)
                    ins.append(remote(bk.at[t, c, pl.ds(mine + block, 2), rr],
                                      ry1.at[t, c, h, j, :, rr], to))
            yield
            for cp in ins:
                cp.wait_recv()
            ins = []
            for h in range(2):
                to, second = ((dev_y3, y3), (dev_y1, y1))[h]
                block = h * 8 + second * 2
                add(block, ry1.at[t, c, h, 1], None)
                ins.append(remote(bk.at[t, c, pl.ds(mine + block, 2), rr],
                                  ry2.at[t, c, h, :, rr], to))
            for h in range(2):
                add(h * 8 + y * 2, ry1.at[t, c, h, 0], None)
            yield
            for cp in ins:
                cp.wait_recv()
            ins = []
            for h in range(2):
                at = mine + h * 8 + y * 2
                bk[t, c, at + 1 - xh, rr, :] += ry2[t, c, h, 1 - xh, rr, :]
                ins.append(remote(bk.at[t, c, at + 1 - xh, rr], rx.at[t, c, h, rr], dev_xh))
                bk[t, c, at + xh, rr, :] += ry2[t, c, h, xh, rr, :]
            yield
            for cp in ins:
                cp.wait_recv()
            x_new = x1 if t == 0 else xo
            ins = []
            for h in range(2):
                vb = mine + h * 8 + y * 2 + xh
                total = bk[t, c, vb, rr, :] + rx[t, c, h, rr, :]
                if ext:
                    csum[t, h] = total[rows:, :]
                if t == 0:
                    old = vol[at_rows, pl.ds(pl.multiple_of(vb * LANES, LANES), LANES)]
                else:
                    old = x1[c, vb]
                x_new[c, vb] = old + RELAXATION * total[:rows, :] / csum[t, h, pl.ds(0, 1), :]
                ins.append(remote(x_new.at[c, vb], x_new.at[c, vb], dev_xh,
                                  x_new.at[c, vb + 1 - 2 * xh]))
            yield
            for cp in ins:
                cp.wait_recv()

            def blocks(h, yb):
                return x_new.at[c, pl.ds(mine + h * 8 + yb * 2, 2)]

            ins = []
            for h in range(2):
                to, got = ((dev_y3, y3), (dev_y1, y1))[h]
                ins.append(remote(blocks(h, y), blocks(h, y), to, blocks(h, got)))
            yield
            for cp in ins:
                cp.wait_recv()
            ins = []
            for h in range(2):
                to, held, got = ((dev_y1, y3, y1), (dev_y3, y1, y3))[h]
                ins.append(remote(blocks(h, y), blocks(h, y), to, blocks(h, got)))
                ins.append(remote(blocks(h, held), blocks(h, held), to, blocks(h, y2)))
            yield
            for cp in ins:
                cp.wait_recv()
            whole = x_new.at[c, pl.ds(mine, half)]
            core_in = remote(whole, whole, dev_core, x_new.at[c, pl.ds(theirs, half)])
            yield
            core_in.wait_recv()
        done = pltpu.make_async_copy(xo.at[c], upd_hbm.at[c],
                                     local_sem.at[steps + chunks + 2 + subsets * chunks + c])
        done.start()
        out_copies.append(done)

    live = [chain(c) for c in range(chunks)]
    while live:
        still = []
        for g in live:
            try:
                next(g)
                still.append(g)
            except StopIteration:
                pass
        live = still
    for cp in out_copies:
        if isinstance(cp, tuple):
            cp[1].wait_recv()
        else:
            cp.wait()
    for cp in pending:
        cp.wait_send()


def per_device(volume, measured, weights, offsets, order):
    subsets, voxels, band = weights.shape
    slices = volume.shape[0]
    cols = measured.shape[2]
    chunks = CHUNKS
    rows = slices // chunks
    r = rows + 8
    nb = band // LANES
    vb = voxels // LANES
    f32 = jnp.float32
    copies = 39 * subsets * chunks
    any_spec = pl.BlockSpec(memory_space=pl.ANY)
    smem = pl.BlockSpec(memory_space=pltpu.SMEM)
    upd, mis = pl.pallas_call(
        lambda *refs: kernel(chunks, *refs),
        out_shape=(jax.ShapeDtypeStruct((chunks, vb, rows, LANES), f32),
                   jax.ShapeDtypeStruct((subsets, chunks, nb, 2, rows, LANES), f32)),
        in_specs=[smem, smem, any_spec, any_spec, any_spec],
        out_specs=(any_spec, any_spec),
        scratch_shapes=[
            pltpu.VMEM((subsets, voxels, band), jnp.bfloat16),
            pltpu.VMEM((slices, voxels), f32),
            pltpu.VMEM((2, subsets, slices, LANES), jnp.bfloat16),
            pltpu.VMEM((rows + 16, band), f32),
            pltpu.VMEM((rows + 16, band), jnp.bfloat16),
            pltpu.VMEM((chunks, vb, rows, LANES), f32),
            pltpu.VMEM((chunks, vb, rows, LANES), f32),
            pltpu.VMEM((subsets, chunks, nb, r, LANES), f32),
            pltpu.VMEM((subsets, chunks, nb, r, LANES), f32),
            pltpu.VMEM((subsets, chunks, nb, rows, LANES), f32),
            pltpu.VMEM((subsets, chunks, nb, rows, LANES), f32),
            pltpu.VMEM((subsets, chunks, 2, rows, LANES), f32),
            pltpu.VMEM((subsets, 2, 8, LANES), f32),
            pltpu.VMEM((subsets, 2, 8, LANES), f32),
            pltpu.VMEM((subsets, chunks, vb, r, LANES), f32),
            pltpu.VMEM((subsets, chunks, vb // 2, r, LANES), f32),
            pltpu.VMEM((subsets, chunks, 2, 2, 2, r, LANES), f32),
            pltpu.VMEM((subsets, chunks, 2, 2, r, LANES), f32),
            pltpu.VMEM((subsets, chunks, 2, r, LANES), f32),
            pltpu.SemaphoreType.DMA((voxels // KB + chunks * 2 + 2 + subsets * chunks,)),
            pltpu.SemaphoreType.DMA((copies,)),
            pltpu.SemaphoreType.DMA((copies,)),
        ],
        compiler_params=pltpu.CompilerParams(
            collective_id=0, has_side_effects=True, vmem_limit_bytes=56 * 2**20),
        name="sart",
    )(order, offsets.reshape(subsets), volume, measured, weights)
    updated = jnp.transpose(upd, (0, 2, 1, 3)).reshape(slices, voxels)
    mis = jnp.where(order[0] == 0, mis, mis[::-1])
    mismatch = jnp.transpose(mis, (0, 1, 4, 3, 2, 5)).reshape(subsets, slices, cols)
    return updated, mismatch


def solution(mesh):
    placed = (
        P(None, "slab"),
        P("view", None, None),
        P("view", "slab", None),
        P("view", "slab"),
        P("view"),
    )
    return jax.shard_map(
        per_device,
        mesh=mesh,
        in_specs=placed,
        out_specs=(P(None, "slab"), P("view", None, None)),
        check_vma=False,
    )
```

time: 340 us -> 134 us (0.39)
  waiting for transfers between devices: 160 us -> 0 us
  Pallas kernels: 0 us -> 124 us
  starting transfers between devices: 48.5 us -> 0 us
  blocking collectives: 37.1 us -> 0 us
  matrix products: 28.3 us -> 0 us
  between operations: 21.9 us -> 1.31 us
  other arithmetic: 20.2 us -> 0.29 us
  local copies, waits for them, and re-layouts: 23.5 us -> 8.5 us
    pallas_call x0 -> x1, Pallas kernels: none -> 124 us  [per_device(): pl.pallas_call(lambda *refs: kernel(chunks, *refs), out_shape=(jax.ShapeD...]
    all_to_all x8 -> x0, waiting for transfers between devices: 85.2 us -> none  [sent_and_summed(): lax.all_to_all(tiles, axis, split_axis=0, concat_axis=0, tiled=True)]
    all_gather x2 -> x0, waiting for transfers between devices: 74.4 us -> none  [per_device(): volume = lax.all_gather(new_part, 'view', axis=1, tiled=True)]
    all_to_all x8 -> x0, starting transfers between devices: 48.5 us -> none  [sent_and_summed(): lax.all_to_all(tiles, axis, split_axis=0, concat_axis=0, tiled=True)]
    all_to_all x2 -> x0, blocking collectives: 37.1 us -> none  [sent_to_all(): lax.all_to_all(jnp.broadcast_to(array[None], (length, *array.shape)), axi...]
    dot_general x4 -> x0, matrix products: 28.3 us -> none  [the longest x2 15.2 us: per_device(): lax.dot_general(band_values, footprint, (((1,), (1,)), ((), ())), preferr...]
    reduce_sum x9 -> x0, other arithmetic: 15.9 us -> none  [the longest x1 13.8 us: per_device(): col_total = jnp.sum(footprint, axis=1, dtype=jnp.float32)]
    dynamic_update_slice x6 -> x0, local copies, waits for them, and re-layouts: 10.9 us -> none  [the longest x2 5.93 us: per_device(): lax.dynamic_update_slice(jnp.zeros((slice_rows, detector_cols), jnp.float...]
  transfers between devices with their start and end apart: 10 -> 0, of which waited for: 6 -> 0; matrix products, arithmetic and copies ran while one was open for 13% -> 0% of each run, Pallas kernels for 0% -> 0%
where the time goes in v1:
time: 134 us
  Pallas kernels  124 us (93%)
  local copies, waits for them, and re-layouts  8.5 us (6%)
    pallas_call x1, Pallas kernels, per_device(): pl.pallas_call(lambda *refs: kernel(chunks, *refs), out_shape=(jax.ShapeD...  124 us
    unnamed x3, local copies, waits for them, and re-layouts  2.98 us
    transpose x1, local copies, waits for them, and re-layouts, per_device(): updated = jnp.transpose(upd, (0, 2, 1, 3)).reshape(slices, voxels)  2.81 us

profile of v1, /device:TPU:1, one launch (start us, length us, event | category | flops | bytes accessed | tf_op | source)
XLA Modules:
  0.0 133.9 jit_solution(274247738527162883)
XLA Ops:
  1.3 123.8 %sart.1 = (f32[2,32,64,128]{3,2,1,0:T(8,128)}, f32[2,2,8,2,64,128]{5,4,3,2,1,0:T(8,128)}) custom-call(s32[2]{0:T(128)} %refs_0_.1, s32[2]{0:T(128)} %bitcast.17, f32[128,4096]{1,0:T(8,128)} %refs_2_.1, bf16[2,128,2048]{2,1,0:T(8,128)(2,1)} %refs_3_.1, bf16[2,4096,1024]{2,1,0:T(8,128)(2,1)} %refs_4_.1), custom_call_target="tpu_custom_call" | custom-call | tf_op jit(solution)/shard_map/sart/pallas_call | solution.py:346
  125.1 2.8 %copy.7 = f32[2,64,32,128]{3,2,1,0:T(8,128)S(1)} copy(f32[2,64,32,128]{3,1,2,0:T(8,128)} %bitcast.15) | data formatting | bytes 4194304 | tf_op jit(solution)/shard_map/transpose | solution.py:380
  127.9 0.0 copy-start
  127.9 3.0 %copy.11 = f32[16,8,32,128]{3,1,2,0:T(8,128)} copy(f32[16,8,32,128]{3,2,1,0:T(8,128)S(1)} %bitcast.13) | data formatting | bytes 4194304
  130.9 0.0 copy-done
  130.9 0.3 fusion
  131.2 1.2 copy.8
  132.4 1.5 %reshape.17 = f32[2,128,2048]{2,1,0:T(8,128)} reshape(f32[2,2,64,2,8,128]{5,4,3,2,1,0:T(8,128)S(1)} %copy.8) | data formatting | bytes 4194304 | tf_op jit(solution)/shard_map/reshape | solution.py:382
Async XLA Ops:
  127.9 3.0 %copy-start = (f32[2,2,8,2,64,128]{5,4,3,2,1,0:T(8,128)S(1)}, f32[2,2,8,2,64,128]{5,4,3,2,1,0:T(8,128)}, u32[]{:S(2)}) copy-start(f32[2,2,8,2,64,128]{5,4,3,2,1,0:T(8,128)} %get-tuple-element.5) | copy-start | bytes 6291460

commit v2 on v1

--- a/solution.py
+++ b/solution.py
@@ -9,12 +9,13 @@
 MESH = pl.DeviceIdType.MESH
 CHUNKS = 2
 LANES = 128
-KB = 512
+KB = 1024
+FAR_FIRST = ((2, 1), (1, 1), (3, 1), (0, 1), (2, 0), (1, 0), (3, 0))
 
 
 def kernel(chunks, order_ref, off_ref, vol_hbm, meas_hbm, w_hbm, upd_hbm, mis_hbm,
            wv, vol, meas, acc, bandb, x1, xo, fs, fr, gs, gr, cor, rsum, csum,
-           bk, rc, ry1, ry2, rx, local_sem, send_sem, recv_sem):
+           bk, rc, rv, obuf, local_sem, send_sem, recv_sem):
     slices, voxels = vol.shape
     rows = slices // chunks
     band = wv.shape[2]
@@ -36,13 +37,11 @@
     def view_dev(other):
         return {"slab": s, "view": other}
 
-    y1 = y + 1 - 2 * lax.rem(y, 2)
-    y3 = 3 - y
-    y2 = lax.rem(y + 2, 4)
     dev_core = view_dev(v + 1 - 2 * core)
-    dev_xh = view_dev(v + 2 - 4 * xh)
-    dev_y1 = view_dev(v + 4 * (y1 - y))
-    dev_y3 = view_dev(v + 4 * (y3 - y))
+
+    def share(dy, dx):
+        return lax.rem(y + dy, 4) * 2 + (1 - xh if dx else xh)
+
     s_mate = s + 1 - 2 * xl
     dev_mate = slab_dev(s_mate)
     dev_z = [None] + [slab_dev(lax.rem(z + k, 4) * 2 + xl) for k in (1, 2, 3)]
@@ -88,9 +87,9 @@
     barrier = pltpu.get_barrier_semaphore()
     for k in range(1, 8):
         pl.semaphore_signal(barrier, inc=1, device_id=slab_dev(lax.rem(s + k, 8)), device_id_type=MESH)
-    for dev in (dev_core, dev_xh, dev_y1, dev_y3):
-        pl.semaphore_signal(barrier, inc=1, device_id=dev, device_id_type=MESH)
-    pl.semaphore_wait(barrier, 11)
+    pl.semaphore_signal(barrier, inc=1, device_id=dev_core, device_id_type=MESH)
+    for dy, dx in FAR_FIRST:
+        pl.semaphore_signal(barrier, inc=1, device_id=view_dev(share(dy, dx) * 2 + core), device_id_type=MESH)
 
     column = lax.broadcasted_iota(jnp.int32, (8, LANES), 1) + s * LANES
     column = column.astype(jnp.float32)
@@ -110,25 +109,34 @@
             shift = jnp.where(off >= band, 0, off)
             if t == 0:
                 vol_copies[c].wait()
-                if c == 0:
-                    for i in range(steps):
-                        w_copy(i).wait()
             acc[pl.ds(0, m), :] = jnp.zeros((m, band), jnp.float32)
 
             def forward(i, carry):
+                at = pl.ds(pl.multiple_of(i * KB, KB), KB)
                 if t == 0:
-                    xk = vol[at_rows, pl.ds(pl.multiple_of(i * KB, KB), KB)]
+                    xk = vol[at_rows, at]
                 else:
                     xk = jnp.concatenate(
                         [x1[c, i * (KB // LANES) + j] for j in range(KB // LANES)], axis=1)
                 xk = xk.astype(jnp.bfloat16)
                 if ext:
                     xk = jnp.concatenate([xk, jnp.ones((2 * ext, KB), jnp.bfloat16)], axis=0)
-                wk = wv[view_t, pl.ds(pl.multiple_of(i * KB, KB), KB), :]
+                if t == 0 and c == 0:
+                    w_copy(i).wait()
+                    wk = jnp.where(view_t == 0, wv[0, at, :], wv[1, at, :])
+                else:
+                    wk = wv[view_t, at, :]
                 acc[pl.ds(0, m), :] += jnp.dot(xk, wk, preferred_element_type=jnp.float32)
                 return carry
 
-            lax.fori_loop(0, steps, forward, 0)
+            if t == 0:
+                lax.fori_loop(0, steps, forward, 0)
+            else:
+                lax.fori_loop(core * (steps // 2), (core + 1) * (steps // 2), forward, 0)
+                core_in.wait_recv()
+                lax.fori_loop((1 - core) * (steps // 2), (2 - core) * (steps // 2), forward, 0)
+            if t == 0 and c == 0:
+                pl.semaphore_wait(barrier, 15)
             folded = pltpu.roll(acc[rr, :], shift, 1)
             if ext:
                 tail = folded[rows:, :]
@@ -172,8 +180,8 @@
             seen_high = meas[1, view_t, at_rows, :].astype(jnp.float32)
             low = (seen_low - low) / rsum[t, 0, pl.ds(0, 1), :]
             high = (seen_high - high) / rsum[t, 1, pl.ds(0, 1), :]
-            cor[t, c, 0] = low
-            cor[t, c, 1] = high
+            cor[t, 0, at_rows, :] = low
+            cor[t, 1, at_rows, :] = high
             arrivals = []
             for k in range(8):
                 piece = jnp.where(masks[k], low, high)
@@ -184,15 +192,17 @@
                     arrivals.append(remote(
                         gs.at[t, c, k], gr.at[t, c, s], slab_dev(lax.rem(s + 8 - k, 8)),
                         gr.at[t, c, lax.rem(s + k, 8)]))
-            own = pltpu.make_async_copy(cor.at[t, c], mis_hbm.at[t, c, s],
-                                        local_sem.at[steps + chunks + 2 + t * chunks + c])
-            own.start()
-            out_copies.append(own)
-            mate_in = remote(cor.at[t, c], mis_hbm.at[t, c, s], dev_mate, mis_hbm.at[t, c, s_mate])
-            for k in (1, 2, 3):
-                far = lax.rem(z + 4 - k, 4) * 2 + xl
-                out_copies.append(("recv", remote(
-                    cor.at[t, c], mis_hbm.at[t, c, s], dev_z[k], mis_hbm.at[t, c, far])))
+            if c == chunks - 1:
+                def cols(slab):
+                    at = pl.ds(pl.multiple_of(slab * LANES, LANES), LANES)
+                    return mis_hbm.at[t, :, :, at]
+                own = pltpu.make_async_copy(cor.at[t], cols(s), local_sem.at[steps + chunks + 2 + t])
+                own.start()
+                out_copies.append(own)
+                mate_in = remote(cor.at[t], cols(s), dev_mate, cols(s_mate))
+                for k in (1, 2, 3):
+                    far = lax.rem(z + 4 - k, 4) * 2 + xl
+                    out_copies.append(("recv", remote(cor.at[t], cols(s), dev_z[k], cols(far))))
             yield
             for cp in arrivals:
                 cp.wait_recv()
@@ -218,96 +228,67 @@
             backward(theirs)
             core_in = remote(bk.at[t, c, pl.ds(theirs, half), rr], rc.at[t, c, :, rr], dev_core)
             backward(mine)
-            mate_in.wait_recv()
-            for k in (1, 2, 3):
-                far = lax.rem(z + 4 - k, 4) * 2 + 1 - xl
-                out_copies.append(("recv", remote(
-                    mis_hbm.at[t, c, s_mate], mis_hbm.at[t, c, s_mate], dev_z[k],
-                    mis_hbm.at[t, c, far])))
+            if c == chunks - 1:
+                mate_in.wait_recv()
+                for k in (1, 2, 3):
+                    far = lax.rem(z + 4 - k, 4) * 2 + 1 - xl
+                    out_copies.append(("recv", remote(cols(s_mate), cols(s_mate), dev_z[k], cols(far))))
             yield
             core_in.wait_recv()
 
-            def add(block, extra, start):
+            def add(q):
                 for j in range(2):
-                    at = mine + block + j
-                    bk[t, c, at, rr, :] += rc[t, c, block + j, rr, :]
-                    if extra is not None:
-                        bk[t, c, at, rr, :] += extra[j, rr, :]
+                    bk[t, c, mine + q * 2 + j, rr, :] += rc[t, c, q * 2 + j, rr, :]
 
             ins = []
-            for h in range(2):
-                to, first = ((dev_y1, y1), (dev_y3, y3))[h]
-                for j, yb in enumerate((first, y2)):
-                    block = h * 8 + yb * 2
-                    add(block, None, None)
-                    ins.append(remote(bk.at[t, c, pl.ds(mine + block, 2), rr],
-                                      ry1.at[t, c, h, j, :, rr], to))
-            yield
-            for cp in ins:
-                cp.wait_recv()
-            ins = []
-            for h in range(2):
-                to, second = ((dev_y3, y3), (dev_y1, y1))[h]
-                block = h * 8 + second * 2
-                add(block, ry1.at[t, c, h, 1], None)
-                ins.append(remote(bk.at[t, c, pl.ds(mine + block, 2), rr],
-                                  ry2.at[t, c, h, :, rr], to))
-            for h in range(2):
-                add(h * 8 + y * 2, ry1.at[t, c, h, 0], None)
-            yield
-            for cp in ins:
-                cp.wait_recv()
-            ins = []
-            for h in range(2):
-                at = mine + h * 8 + y * 2
-                bk[t, c, at + 1 - xh, rr, :] += ry2[t, c, h, 1 - xh, rr, :]
-                ins.append(remote(bk.at[t, c, at + 1 - xh, rr], rx.at[t, c, h, rr], dev_xh))
-                bk[t, c, at + xh, rr, :] += ry2[t, c, h, xh, rr, :]
+            for k, (dy, dx) in enumerate(FAR_FIRST):
+                q = share(dy, dx)
+                add(q)
+                ins.append(remote(bk.at[t, c, pl.ds(mine + q * 2, 2), rr], rv.at[t, c, k, :, rr],
+                                  view_dev(q * 2 + core)))
+            q = share(0, 0)
+            add(q)
             yield
             for cp in ins:
                 cp.wait_recv()
             x_new = x1 if t == 0 else xo
-            ins = []
-            for h in range(2):
-                vb = mine + h * 8 + y * 2 + xh
-                total = bk[t, c, vb, rr, :] + rx[t, c, h, rr, :]
+            for j in range(2):
+                vb = mine + q * 2 + j
+                total = bk[t, c, vb, rr, :]
+                for k in range(7):
+                    total += rv[t, c, k, j, rr, :]
                 if ext:
-                    csum[t, h] = total[rows:, :]
+                    csum[t, j] = total[rows:, :]
                 if t == 0:
                     old = vol[at_rows, pl.ds(pl.multiple_of(vb * LANES, LANES), LANES)]
                 else:
                     old = x1[c, vb]
-                x_new[c, vb] = old + RELAXATION * total[:rows, :] / csum[t, h, pl.ds(0, 1), :]
-                ins.append(remote(x_new.at[c, vb], x_new.at[c, vb], dev_xh,
-                                  x_new.at[c, vb + 1 - 2 * xh]))
-            yield
-            for cp in ins:
-                cp.wait_recv()
-
-            def blocks(h, yb):
-                return x_new.at[c, pl.ds(mine + h * 8 + yb * 2, 2)]
-
+                x_new[c, vb] = old + RELAXATION * total[:rows, :] / csum[t, j, pl.ds(0, 1), :]
             ins = []
-            for h in range(2):
-                to, got = ((dev_y3, y3), (dev_y1, y1))[h]
-                ins.append(remote(blocks(h, y), blocks(h, y), to, blocks(h, got)))
-            yield
-            for cp in ins:
-                cp.wait_recv()
-            ins = []
-            for h in range(2):
-                to, held, got = ((dev_y1, y3, y1), (dev_y3, y1, y3))[h]
-                ins.append(remote(blocks(h, y), blocks(h, y), to, blocks(h, got)))
-                ins.append(remote(blocks(h, held), blocks(h, held), to, blocks(h, y2)))
+
+            def piece(q):
+                return x_new.at[c, pl.ds(mine + q * 2, 2)]
+
+            for dy, dx in FAR_FIRST:
+                to = share(dy, dx)
+                ins.append(remote(piece(q), piece(q), view_dev(to * 2 + core), piece(share(4 - dy, dx))))
             yield
             for cp in ins:
                 cp.wait_recv()
             whole = x_new.at[c, pl.ds(mine, half)]
             core_in = remote(whole, whole, dev_core, x_new.at[c, pl.ds(theirs, half)])
             yield
-            core_in.wait_recv()
-        done = pltpu.make_async_copy(xo.at[c], upd_hbm.at[c],
-                                     local_sem.at[steps + chunks + 2 + subsets * chunks + c])
+
+        def lay_out(base):
+            for j in range(half):
+                at = pl.ds(pl.multiple_of((base + j) * LANES, LANES), LANES)
+                obuf[at_rows, at] = xo[c, base + j]
+
+        lay_out(mine)
+        core_in.wait_recv()
+        lay_out(theirs)
+        done = pltpu.make_async_copy(obuf.at[at_rows, :], upd_hbm.at[at_rows, :],
+                                     local_sem.at[steps + chunks + 2 + subsets + c])
         done.start()
         out_copies.append(done)
 
@@ -340,13 +321,13 @@
     nb = band // LANES
     vb = voxels // LANES
     f32 = jnp.float32
-    copies = 39 * subsets * chunks
+    copies = (7 * 4 + 2) * subsets * chunks + 7 * subsets
     any_spec = pl.BlockSpec(memory_space=pl.ANY)
     smem = pl.BlockSpec(memory_space=pltpu.SMEM)
     upd, mis = pl.pallas_call(
         lambda *refs: kernel(chunks, *refs),
-        out_shape=(jax.ShapeDtypeStruct((chunks, vb, rows, LANES), f32),
-                   jax.ShapeDtypeStruct((subsets, chunks, nb, 2, rows, LANES), f32)),
+        out_shape=(jax.ShapeDtypeStruct((slices, voxels), f32),
+                   jax.ShapeDtypeStruct((subsets, 2, slices, band), f32)),
         in_specs=[smem, smem, any_spec, any_spec, any_spec],
         out_specs=(any_spec, any_spec),
         scratch_shapes=[
@@ -361,15 +342,14 @@
             pltpu.VMEM((subsets, chunks, nb, r, LANES), f32),
             pltpu.VMEM((subsets, chunks, nb, rows, LANES), f32),
             pltpu.VMEM((subsets, chunks, nb, rows, LANES), f32),
-            pltpu.VMEM((subsets, chunks, 2, rows, LANES), f32),
+            pltpu.VMEM((subsets, 2, slices, LANES), f32),
             pltpu.VMEM((subsets, 2, 8, LANES), f32),
             pltpu.VMEM((subsets, 2, 8, LANES), f32),
             pltpu.VMEM((subsets, chunks, vb, r, LANES), f32),
             pltpu.VMEM((subsets, chunks, vb // 2, r, LANES), f32),
-            pltpu.VMEM((subsets, chunks, 2, 2, 2, r, LANES), f32),
-            pltpu.VMEM((subsets, chunks, 2, 2, r, LANES), f32),
-            pltpu.VMEM((subsets, chunks, 2, r, LANES), f32),
-            pltpu.SemaphoreType.DMA((voxels // KB + chunks * 2 + 2 + subsets * chunks,)),
+            pltpu.VMEM((subsets, chunks, 7, 2, r, LANES), f32),
+            pltpu.VMEM((slices, voxels), f32),
+            pltpu.SemaphoreType.DMA((voxels // KB + chunks * 2 + 2 + subsets,)),
             pltpu.SemaphoreType.DMA((copies,)),
             pltpu.SemaphoreType.DMA((copies,)),
         ],
@@ -377,10 +357,39 @@
             collective_id=0, has_side_effects=True, vmem_limit_bytes=56 * 2**20),
         name="sart",
     )(order, offsets.reshape(subsets), volume, measured, weights)
-    updated = jnp.transpose(upd, (0, 2, 1, 3)).reshape(slices, voxels)
-    mis = jnp.where(order[0] == 0, mis, mis[::-1])
-    mismatch = jnp.transpose(mis, (0, 1, 4, 3, 2, 5)).reshape(subsets, slices, cols)
-    return updated, mismatch
+    return place(order, upd, mis)
+
+
+def place_kernel(order_ref, upd_hbm, mis_hbm, out_upd, out_mis, sem):
+    band = mis_hbm.shape[3]
+    rows = upd_hbm.shape[0] // 4
+    copies = []
+    for i in range(4):
+        at = pl.ds(i * rows, rows)
+        copies.append(pltpu.make_async_copy(upd_hbm.at[at, :], out_upd.at[at, :], sem.at[i]))
+    for t in range(mis_hbm.shape[0]):
+        view = order_ref[t]
+        for hi in range(2):
+            copies.append(pltpu.make_async_copy(
+                mis_hbm.at[t, hi], out_mis.at[view, :, pl.ds(hi * band, band)], sem.at[4 + t * 2 + hi]))
+    for cp in copies:
+        cp.start()
+    for cp in copies:
+        cp.wait()
+
+
+def place(order, upd, mis):
+    subsets, _, slices, band = mis.shape
+    any_spec = pl.BlockSpec(memory_space=pl.ANY)
+    return pl.pallas_call(
+        place_kernel,
+        out_shape=(jax.ShapeDtypeStruct(upd.shape, upd.dtype),
+                   jax.ShapeDtypeStruct((subsets, slices, 2 * band), mis.dtype)),
+        in_specs=[pl.BlockSpec(memory_space=pltpu.SMEM), any_spec, any_spec],
+        out_specs=(any_spec, any_spec),
+        scratch_shapes=[pltpu.SemaphoreType.DMA((8,))],
+        name="place",
+    )(order, upd, mis)
 
 
 def solution(mesh):

time: 134 us -> 239 us (1.78)
  Pallas kernels: 124 us -> 238 us
  local copies, waits for them, and re-layouts: 8.5 us -> 0 us
    pallas_call x0 -> x1, Pallas kernels: none -> 129 us  [place(): pl.pallas_call(place_kernel, out_shape=(jax.ShapeDtypeStruct(upd.shape, u...]
    pallas_call x1, Pallas kernels: 124 us -> 109 us  [per_device(): pl.pallas_call(lambda *refs: kernel(chunks, *refs), out_shape=(jax.ShapeD...]
    transpose x2 -> x0, local copies, waits for them, and re-layouts: 4.03 us -> none  [the longest x1 2.81 us: per_device(): updated = jnp.transpose(upd, (0, 2, 1, 3)).reshape(slices, voxels)]
    unnamed x3 -> x0, local copies, waits for them, and re-layouts: 2.98 us -> none
where the time goes in v2:
time: 239 us
  Pallas kernels  238 us (100%)
    pallas_call x1, Pallas kernels, place(): pl.pallas_call(place_kernel, out_shape=(jax.ShapeDtypeStruct(upd.shape, u...  129 us
    pallas_call x1, Pallas kernels, per_device(): pl.pallas_call(lambda *refs: kernel(chunks, *refs), out_shape=(jax.ShapeD...  109 us

profile of v2, /device:TPU:1, one launch (start us, length us, event | category | flops | bytes accessed | tf_op | source)
XLA Modules:
  0.0 239.0 jit_solution(15235640654008493358)
XLA Ops:
  0.6 109.4 %sart.1 = (f32[128,4096]{1,0:T(8,128)}, f32[2,2,128,1024]{3,2,1,0:T(8,128)}) custom-call(s32[2]{0:T(128)} %order_ref.1, s32[2]{0:T(128)} %bitcast.1, f32[128,4096]{1,0:T(8,128)} %refs_2_.1, bf16[2,128,2048]{2,1,0:T(8,128)(2,1)} %refs_3_.1, bf16[2,4096,1024]{2,1,0:T(8,128)(2,1)} %refs_4_.1), custom_call_target="tpu_custom_call" | custom-call | tf_op jit(solution)/shard_map/sart/pallas_call | solution.py:327
  110.1 128.9 %place.1 = (f32[128,4096]{1,0:T(8,128)}, f32[2,128,2048]{2,1,0:T(8,128)}) custom-call(s32[2]{0:T(128)} %order_ref.1, f32[128,4096]{1,0:T(8,128)} %get-tuple-element.4.upd_hbm, f32[2,2,128,1024]{3,2,1,0:T(8,128)} %get-tuple-element.5.mis_hbm), custom_call_target="tpu_custom_call" | custom-call | tf_op jit(solution)/shard_map/place/pallas_call | solution.py:384

commit v3 on v2

--- a/solution.py
+++ b/solution.py
@@ -10,12 +10,12 @@
 CHUNKS = 2
 LANES = 128
 KB = 1024
-FAR_FIRST = ((2, 1), (1, 1), (3, 1), (0, 1), (2, 0), (1, 0), (3, 0))
+ORDER = (0, 1) + (0, 1, 0, 1, 0, 0, 1, 1, 0, 1, 0, 1, 0, 1, 0, 1, 0, 1) * 2
 
 
 def kernel(chunks, order_ref, off_ref, vol_hbm, meas_hbm, w_hbm, upd_hbm, mis_hbm,
            wv, vol, meas, acc, bandb, x1, xo, fs, fr, gs, gr, cor, rsum, csum,
-           bk, rc, rv, obuf, local_sem, send_sem, recv_sem):
+           bk, rc, ry0, rx0, ry1, rx1, obuf, mis, local_sem, send_sem, recv_sem):
     slices, voxels = vol.shape
     rows = slices // chunks
     band = wv.shape[2]
@@ -39,8 +39,13 @@
 
     dev_core = view_dev(v + 1 - 2 * core)
 
-    def share(dy, dx):
-        return lax.rem(y + dy, 4) * 2 + (1 - xh if dx else xh)
+    dev_x = view_dev(v + 2 - 4 * xh)
+
+    def turned(dy):
+        return lax.rem(y + dy, 4)
+
+    def dev_y(dy):
+        return view_dev(v + 4 * (turned(dy) - y))
 
     s_mate = s + 1 - 2 * xl
     dev_mate = slab_dev(s_mate)
@@ -88,13 +93,14 @@
     for k in range(1, 8):
         pl.semaphore_signal(barrier, inc=1, device_id=slab_dev(lax.rem(s + k, 8)), device_id_type=MESH)
     pl.semaphore_signal(barrier, inc=1, device_id=dev_core, device_id_type=MESH)
-    for dy, dx in FAR_FIRST:
-        pl.semaphore_signal(barrier, inc=1, device_id=view_dev(share(dy, dx) * 2 + core), device_id_type=MESH)
+    for dev in (dev_x, dev_y(1), dev_y(2), dev_y(3)):
+        pl.semaphore_signal(barrier, inc=1, device_id=dev, device_id_type=MESH)
 
     column = lax.broadcasted_iota(jnp.int32, (8, LANES), 1) + s * LANES
     column = column.astype(jnp.float32)
 
     out_copies = []
+    gathered = [[], []]
 
     def chain(c):
         at_rows = pl.ds(c * rows, rows)
@@ -109,7 +115,6 @@
             shift = jnp.where(off >= band, 0, off)
             if t == 0:
                 vol_copies[c].wait()
-            acc[pl.ds(0, m), :] = jnp.zeros((m, band), jnp.float32)
 
             def forward(i, carry):
                 at = pl.ds(pl.multiple_of(i * KB, KB), KB)
@@ -126,18 +131,29 @@
                     wk = jnp.where(view_t == 0, wv[0, at, :], wv[1, at, :])
                 else:
                     wk = wv[view_t, at, :]
-                acc[pl.ds(0, m), :] += jnp.dot(xk, wk, preferred_element_type=jnp.float32)
+                acc[c, pl.ds(0, m), :] += jnp.dot(xk, wk, preferred_element_type=jnp.float32)
                 return carry
 
+            acc[c, pl.ds(0, m), :] = jnp.zeros((m, band), jnp.float32)
             if t == 0:
                 lax.fori_loop(0, steps, forward, 0)
             else:
-                lax.fori_loop(core * (steps // 2), (core + 1) * (steps // 2), forward, 0)
-                core_in.wait_recv()
-                lax.fori_loop((1 - core) * (steps // 2), (2 - core) * (steps // 2), forward, 0)
+
+                def joined(i, carry):
+                    return forward(lax.rem(core + i // 2, 2) * 2 + lax.rem(1 + i, 2), carry)
+
+                lax.fori_loop(0, 1, joined, 0)
+                pass_on_rest()
+                lax.fori_loop(1, 2, joined, 0)
+                yield
+                core_in[0].wait_recv()
+                core_in[1].wait_recv()
+                lax.fori_loop(2, 3, joined, 0)
+                core_in[2].wait_recv()
+                lax.fori_loop(3, 4, joined, 0)
             if t == 0 and c == 0:
-                pl.semaphore_wait(barrier, 15)
-            folded = pltpu.roll(acc[rr, :], shift, 1)
+                pl.semaphore_wait(barrier, 12)
+            folded = pltpu.roll(acc[c, rr, :], shift, 1)
             if ext:
                 tail = folded[rows:, :]
                 kind = lax.broadcasted_iota(jnp.int32, tail.shape, 0)
@@ -192,31 +208,31 @@
                     arrivals.append(remote(
                         gs.at[t, c, k], gr.at[t, c, s], slab_dev(lax.rem(s + 8 - k, 8)),
                         gr.at[t, c, lax.rem(s + k, 8)]))
+            yield
+            for cp in arrivals:
+                cp.wait_recv()
             if c == chunks - 1:
                 def cols(slab):
                     at = pl.ds(pl.multiple_of(slab * LANES, LANES), LANES)
-                    return mis_hbm.at[t, :, :, at]
-                own = pltpu.make_async_copy(cor.at[t], cols(s), local_sem.at[steps + chunks + 2 + t])
-                own.start()
-                out_copies.append(own)
+                    return mis.at[t, :, :, at]
+                at = pl.ds(pl.multiple_of(s * LANES, LANES), LANES)
+                for hi in range(2):
+                    mis[t, hi, :, at] = cor[t, hi]
                 mate_in = remote(cor.at[t], cols(s), dev_mate, cols(s_mate))
                 for k in (1, 2, 3):
                     far = lax.rem(z + 4 - k, 4) * 2 + xl
-                    out_copies.append(("recv", remote(cor.at[t], cols(s), dev_z[k], cols(far))))
-            yield
-            for cp in arrivals:
-                cp.wait_recv()
+                    gathered[t].append((remote(cor.at[t], cols(s), dev_z[k], cols(far))))
             g = jnp.concatenate([gr[t, c, b] for b in range(nb)], axis=1)
             g = pltpu.roll(g, jnp.where(shift == 0, 0, band - shift), 1).astype(jnp.bfloat16)
-            bandb[only, :] = g
+            bandb[c, only, :] = g
             if ext:
-                bandb[pl.ds(rows, 2 * ext), :] = jnp.ones((2 * ext, band), jnp.bfloat16)
+                bandb[c, pl.ds(rows, 2 * ext), :] = jnp.ones((2 * ext, band), jnp.bfloat16)
 
             def backward(base):
                 def step(n, carry):
                     vb = base + n * (KB // LANES)
                     wk = wv[view_t, pl.ds(pl.multiple_of(vb * LANES, LANES), KB), :]
-                    res = lax.dot_general(bandb[pl.ds(0, m), :], wk, (((1,), (1,)), ((), ())),
+                    res = lax.dot_general(bandb[c, pl.ds(0, m), :], wk, (((1,), (1,)), ((), ())),
                                           preferred_element_type=jnp.float32)
                     for j in range(KB // LANES):
                         bk[t, c, vb + j, rr, :] = res[:r, j * LANES:(j + 1) * LANES]
@@ -227,36 +243,62 @@
             mine = core * half
             backward(theirs)
             core_in = remote(bk.at[t, c, pl.ds(theirs, half), rr], rc.at[t, c, :, rr], dev_core)
+            yield
             backward(mine)
+            yield
             if c == chunks - 1:
                 mate_in.wait_recv()
                 for k in (1, 2, 3):
                     far = lax.rem(z + 4 - k, 4) * 2 + 1 - xl
-                    out_copies.append(("recv", remote(cols(s_mate), cols(s_mate), dev_z[k], cols(far))))
-            yield
+                    gathered[t].append((remote(cols(s_mate), cols(s_mate), dev_z[k], cols(far))))
             core_in.wait_recv()
 
-            def add(q):
+            def add(block, *others):
+                total = bk[t, c, mine + block, rr, :]
+                for other in others:
+                    total += other[...]
+                bk[t, c, mine + block, rr, :] = total
+
+            def theirs_of(block):
+                return rc.at[t, c, block, rr]
+
+            other_x = 8 + (1 - xh) * 4
+            own_x = 8 + xh * 4
+            ins_y, ins_x = [], []
+            for j in range(4):
+                add(other_x + j, theirs_of(other_x + j))
+            ins_x.append(remote(bk.at[t, c, pl.ds(mine + other_x, 4), rr], rx1.at[t, c, :, rr], dev_x))
+            for k in (2, 1, 3):
+                block = turned(k) * 2
                 for j in range(2):
-                    bk[t, c, mine + q * 2 + j, rr, :] += rc[t, c, q * 2 + j, rr, :]
-
-            ins = []
-            for k, (dy, dx) in enumerate(FAR_FIRST):
-                q = share(dy, dx)
-                add(q)
-                ins.append(remote(bk.at[t, c, pl.ds(mine + q * 2, 2), rr], rv.at[t, c, k, :, rr],
-                                  view_dev(q * 2 + core)))
-            q = share(0, 0)
-            add(q)
-            yield
-            for cp in ins:
-                cp.wait_recv()
+                    add(block + j, theirs_of(block + j))
+                ins_y.append(remote(bk.at[t, c, pl.ds(mine + block, 2), rr],
+                                    ry0.at[t, c, k - 1, :, rr], dev_y(k)))
+            yield
+            for cp in ins_x:
+                cp.wait_recv()
+            last_x, last_y = [], []
+            for k in (2, 1, 3, 0):
+                block = own_x + turned(k)
+                add(block, theirs_of(block), rx1.at[t, c, turned(k), rr])
+                if k:
+                    last_y.append(remote(bk.at[t, c, mine + block, rr], ry1.at[t, c, k - 1, rr], dev_y(k)))
+            for cp in ins_y:
+                cp.wait_recv()
+            for far in (1, 0):
+                at = 1 - xh if far else xh
+                block = y * 2 + at
+                add(block, theirs_of(block), *[ry0.at[t, c, k, at, rr] for k in range(3)])
+                if far:
+                    last_x.append(remote(bk.at[t, c, mine + block, rr], rx0.at[t, c, rr], dev_x))
+            yield
             x_new = x1 if t == 0 else xo
-            for j in range(2):
-                vb = mine + q * 2 + j
+
+            def renew(block, j, *others):
+                vb = mine + block
                 total = bk[t, c, vb, rr, :]
-                for k in range(7):
-                    total += rv[t, c, k, j, rr, :]
+                for other in others:
+                    total += other[...]
                 if ext:
                     csum[t, j] = total[rows:, :]
                 if t == 0:
@@ -264,28 +306,57 @@
                 else:
                     old = x1[c, vb]
                 x_new[c, vb] = old + RELAXATION * total[:rows, :] / csum[t, j, pl.ds(0, 1), :]
-            ins = []
-
-            def piece(q):
-                return x_new.at[c, pl.ds(mine + q * 2, 2)]
-
-            for dy, dx in FAR_FIRST:
-                to = share(dy, dx)
-                ins.append(remote(piece(q), piece(q), view_dev(to * 2 + core), piece(share(4 - dy, dx))))
-            yield
-            for cp in ins:
-                cp.wait_recv()
-            whole = x_new.at[c, pl.ds(mine, half)]
-            core_in = remote(whole, whole, dev_core, x_new.at[c, pl.ds(theirs, half)])
-            yield
+
+            def send(at, dev, arrives):
+                return remote(at, at, dev, arrives)
+
+            def span(block, count, x_new=x_new):
+                return x_new.at[c, pl.ds(mine + block, count)]
+
+            for cp in last_y:
+                cp.wait_recv()
+            renew(own_x + y, 1, *[ry1.at[t, c, k, rr] for k in range(3)])
+            ins_y = [send(span(own_x + y, 1), dev_y(k), span(own_x + turned(4 - k), 1)) for k in (2, 1, 3)]
+            for cp in last_x:
+                cp.wait_recv()
+            renew(y * 2 + xh, 0, rx0.at[t, c, rr])
+            ins_x = [send(span(y * 2 + xh, 1), dev_x, span(y * 2 + 1 - xh, 1))]
+            yield
+            for cp in ins_y:
+                cp.wait_recv()
+            last_x = [send(span(own_x, 4), dev_x, span(other_x, 4))]
+            for cp in ins_x:
+                cp.wait_recv()
+            last_y = [send(span(y * 2, 2), dev_y(k), span(turned(4 - k) * 2, 2)) for k in (2, 1, 3)]
+
+            def pass_on(block, count, x_new=x_new):
+                return send(x_new.at[c, pl.ds(mine + block, count)], dev_core,
+                            x_new.at[c, pl.ds(theirs + block, count)])
+
+            core_in = [pass_on(own_x, 4)]
+            yield
+            for cp in last_x:
+                cp.wait_recv()
+            core_in.append(pass_on(other_x, 4))
+
+            def pass_on_rest(last_y=last_y, core_in=core_in, pass_on=pass_on):
+                for cp in last_y:
+                    cp.wait_recv()
+                core_in.append(pass_on(0, 8))
 
         def lay_out(base):
-            for j in range(half):
+            for j in range(half // 2):
                 at = pl.ds(pl.multiple_of((base + j) * LANES, LANES), LANES)
                 obuf[at_rows, at] = xo[c, base + j]
 
+        lay_out(mine + 8)
+        pass_on_rest()
         lay_out(mine)
-        core_in.wait_recv()
+        yield
+        core_in[0].wait_recv()
+        core_in[1].wait_recv()
+        lay_out(theirs + 8)
+        core_in[2].wait_recv()
         lay_out(theirs)
         done = pltpu.make_async_copy(obuf.at[at_rows, :], upd_hbm.at[at_rows, :],
                                      local_sem.at[steps + chunks + 2 + subsets + c])
@@ -293,20 +364,16 @@
         out_copies.append(done)
 
     live = [chain(c) for c in range(chunks)]
-    while live:
-        still = []
-        for g in live:
-            try:
-                next(g)
-                still.append(g)
-            except StopIteration:
-                pass
-        live = still
+    for c in ORDER:
+        next(live[c], None)
+    for t in range(subsets):
+        for cp in gathered[t]:
+            cp.wait_recv()
+        cp = pltpu.make_async_copy(mis.at[t], mis_hbm.at[t], local_sem.at[steps + chunks + 2 + t])
+        cp.start()
+        out_copies.append(cp)
     for cp in out_copies:
-        if isinstance(cp, tuple):
-            cp[1].wait_recv()
-        else:
-            cp.wait()
+        cp.wait()
     for cp in pending:
         cp.wait_send()
 
@@ -321,7 +388,7 @@
     nb = band // LANES
     vb = voxels // LANES
     f32 = jnp.float32
-    copies = (7 * 4 + 2) * subsets * chunks + 7 * subsets
+    copies = 34 * subsets * chunks + 7 * subsets
     any_spec = pl.BlockSpec(memory_space=pl.ANY)
     smem = pl.BlockSpec(memory_space=pltpu.SMEM)
     upd, mis = pl.pallas_call(
@@ -334,8 +401,8 @@
             pltpu.VMEM((subsets, voxels, band), jnp.bfloat16),
             pltpu.VMEM((slices, voxels), f32),
             pltpu.VMEM((2, subsets, slices, LANES), jnp.bfloat16),
-            pltpu.VMEM((rows + 16, band), f32),
-            pltpu.VMEM((rows + 16, band), jnp.bfloat16),
+            pltpu.VMEM((chunks, rows + 16, band), f32),
+            pltpu.VMEM((chunks, rows + 16, band), jnp.bfloat16),
             pltpu.VMEM((chunks, vb, rows, LANES), f32),
             pltpu.VMEM((chunks, vb, rows, LANES), f32),
             pltpu.VMEM((subsets, chunks, nb, r, LANES), f32),
@@ -347,8 +414,12 @@
             pltpu.VMEM((subsets, 2, 8, LANES), f32),
             pltpu.VMEM((subsets, chunks, vb, r, LANES), f32),
             pltpu.VMEM((subsets, chunks, vb // 2, r, LANES), f32),
-            pltpu.VMEM((subsets, chunks, 7, 2, r, LANES), f32),
+            pltpu.VMEM((subsets, chunks, 3, 2, r, LANES), f32),
+            pltpu.VMEM((subsets, chunks, r, LANES), f32),
+            pltpu.VMEM((subsets, chunks, 3, r, LANES), f32),
+            pltpu.VMEM((subsets, chunks, 4, r, LANES), f32),
             pltpu.VMEM((slices, voxels), f32),
+            pltpu.VMEM((subsets, 2, slices, band), f32),
             pltpu.SemaphoreType.DMA((voxels // KB + chunks * 2 + 2 + subsets,)),
             pltpu.SemaphoreType.DMA((copies,)),
             pltpu.SemaphoreType.DMA((copies,)),
@@ -360,21 +431,25 @@
     return place(order, upd, mis)
 
 
-def place_kernel(order_ref, upd_hbm, mis_hbm, out_upd, out_mis, sem):
-    band = mis_hbm.shape[3]
-    rows = upd_hbm.shape[0] // 4
-    copies = []
+def place_kernel(order_ref, upd_hbm, mis_hbm, out_upd, out_mis, upd, mis, sem):
+    band = mis.shape[3]
+    rows = upd.shape[0] // 4
+    moves = []
+    for t in range(mis.shape[0]):
+        view = order_ref[t]
+        for hi in range(2):
+            moves.append((mis_hbm.at[t, hi], mis.at[t, hi], out_mis.at[view, :, pl.ds(hi * band, band)]))
     for i in range(4):
         at = pl.ds(i * rows, rows)
-        copies.append(pltpu.make_async_copy(upd_hbm.at[at, :], out_upd.at[at, :], sem.at[i]))
-    for t in range(mis_hbm.shape[0]):
-        view = order_ref[t]
-        for hi in range(2):
-            copies.append(pltpu.make_async_copy(
-                mis_hbm.at[t, hi], out_mis.at[view, :, pl.ds(hi * band, band)], sem.at[4 + t * 2 + hi]))
-    for cp in copies:
+        moves.append((upd_hbm.at[at, :], upd.at[at, :], out_upd.at[at, :]))
+    loads = [pltpu.make_async_copy(a, b, sem.at[0, i]) for i, (a, b, _) in enumerate(moves)]
+    stores = [pltpu.make_async_copy(b, c, sem.at[1, i]) for i, (_, b, c) in enumerate(moves)]
+    for cp in loads:
         cp.start()
-    for cp in copies:
+    for load, store in zip(loads, stores):
+        load.wait()
+        store.start()
+    for cp in stores:
         cp.wait()
 
 
@@ -387,7 +462,8 @@
                    jax.ShapeDtypeStruct((subsets, slices, 2 * band), mis.dtype)),
         in_specs=[pl.BlockSpec(memory_space=pltpu.SMEM), any_spec, any_spec],
         out_specs=(any_spec, any_spec),
-        scratch_shapes=[pltpu.SemaphoreType.DMA((8,))],
+        scratch_shapes=[pltpu.VMEM(upd.shape, upd.dtype), pltpu.VMEM(mis.shape, mis.dtype),
+                        pltpu.SemaphoreType.DMA((2, 8))],
         name="place",
     )(order, upd, mis)
 

time: 239 us -> 105 us (0.44)
  Pallas kernels: 238 us -> 105 us
    pallas_call x1, Pallas kernels: 129 us -> 4.24 us  [place(): pl.pallas_call(place_kernel, out_shape=(jax.ShapeDtypeStruct(upd.shape, u...]
    pallas_call x1, Pallas kernels: 109 us -> 100 us  [per_device(): pl.pallas_call(lambda *refs: kernel(chunks, *refs), out_shape=(jax.ShapeD...]
where the time goes in v3:
time: 105 us
  Pallas kernels  105 us (100%)
    pallas_call x1, Pallas kernels, per_device(): pl.pallas_call(lambda *refs: kernel(chunks, *refs), out_shape=(jax.ShapeD...  100 us
    pallas_call x1, Pallas kernels, place(): pl.pallas_call(place_kernel, out_shape=(jax.ShapeDtypeStruct(upd.shape, u...  4.24 us

profile of v3, /device:TPU:1, one launch (start us, length us, event | category | flops | bytes accessed | tf_op | source)
XLA Modules:
  0.0 105.4 jit_solution(2623028726468138295)
XLA Ops:
  0.6 100.5 %sart.1 = (f32[128,4096]{1,0:T(8,128)}, f32[2,2,128,1024]{3,2,1,0:T(8,128)}) custom-call(s32[2]{0:T(128)} %order_ref.1, s32[2]{0:T(128)} %bitcast.1, f32[128,4096]{1,0:T(8,128)} %refs_2_.1, bf16[2,128,2048]{2,1,0:T(8,128)(2,1)} %refs_3_.1, bf16[2,4096,1024]{2,1,0:T(8,128)(2,1)} %refs_4_.1), custom_call_target="tpu_custom_call" | custom-call | tf_op jit(solution)/shard_map/sart/pallas_call | solution.py:394
  101.1 4.2 %place.1 = (f32[128,4096]{1,0:T(8,128)}, f32[2,128,2048]{2,1,0:T(8,128)}) custom-call(s32[2]{0:T(128)} %order_ref.1, f32[128,4096]{1,0:T(8,128)} %get-tuple-element.4.upd_hbm, f32[2,2,128,1024]{3,2,1,0:T(8,128)} %get-tuple-element.5.mis_hbm), custom_call_target="tpu_custom_call" | custom-call | tf_op jit(solution)/shard_map/place/pallas_call | solution.py:459

commit v4 on v3

--- a/solution.py
+++ b/solution.py
@@ -10,12 +10,13 @@
 CHUNKS = 2
 LANES = 128
 KB = 1024
-ORDER = (0, 1) + (0, 1, 0, 1, 0, 0, 1, 1, 0, 1, 0, 1, 0, 1, 0, 1, 0, 1) * 2
-
-
-def kernel(chunks, order_ref, off_ref, vol_hbm, meas_hbm, w_hbm, upd_hbm, mis_hbm,
+SLAB_PEERS = ((2, 1), (1, 1), (3, 1), (2, 0), (1, 0), (3, 0), (0, 1))
+ORDER = (0, 1) + (0, 1, 0, 1, 0, 0, 1, 1, 0, 1, 0, 1, 0, 1, 0, 0, 1, 1) * 2
+
+
+def kernel(chunks, order_ref, off_ref, vol_hbm, meas_hbm, w_hbm, obuf, mis,
            wv, vol, meas, acc, bandb, x1, xo, fs, fr, gs, gr, cor, rsum, csum,
-           bk, rc, ry0, rx0, ry1, rx1, obuf, mis, local_sem, send_sem, recv_sem):
+           bk, rc, ry0, rx0, ry1, rx1, local_sem, send_sem, recv_sem):
     slices, voxels = vol.shape
     rows = slices // chunks
     band = wv.shape[2]
@@ -49,6 +50,10 @@
 
     s_mate = s + 1 - 2 * xl
     dev_mate = slab_dev(s_mate)
+
+    def across(dz, dx):
+        return lax.rem(z + dz, 4) * 2 + (1 - xl if dx else xl)
+
     dev_z = [None] + [slab_dev(lax.rem(z + k, 4) * 2 + xl) for k in (1, 2, 3)]
 
     used = [0]
@@ -163,8 +168,8 @@
                 if ext:
                     fs[t, c, b, pl.ds(rows, ext), :] = tail[:, b * LANES:(b + 1) * LANES]
             arrivals = []
-            for k in range(1, 8):
-                peer = lax.rem(s + k, 8)
+            for k, (dz, dx) in enumerate(SLAB_PEERS, 1):
+                peer = across(dz, dx)
                 arrivals.append(remote(fs.at[t, c, peer, rr], fr.at[t, c, k, rr], slab_dev(peer)))
             yield
             fr[t, c, 0, rr, :] = fs[t, c, s, rr, :]
@@ -199,15 +204,12 @@
             cor[t, 0, at_rows, :] = low
             cor[t, 1, at_rows, :] = high
             arrivals = []
-            for k in range(8):
-                piece = jnp.where(masks[k], low, high)
-                if k == 0:
-                    gr[t, c, s] = piece
-                else:
-                    gs[t, c, k] = piece
-                    arrivals.append(remote(
-                        gs.at[t, c, k], gr.at[t, c, s], slab_dev(lax.rem(s + 8 - k, 8)),
-                        gr.at[t, c, lax.rem(s + k, 8)]))
+            for k, (dz, dx) in enumerate(SLAB_PEERS, 1):
+                gs[t, c, k] = jnp.where(masks[k], low, high)
+                arrivals.append(remote(
+                    gs.at[t, c, k], gr.at[t, c, s], slab_dev(across(4 - dz, dx)),
+                    gr.at[t, c, across(dz, dx)]))
+            gr[t, c, s] = jnp.where(masks[0], low, high)
             yield
             for cp in arrivals:
                 cp.wait_recv()
@@ -218,7 +220,6 @@
                 at = pl.ds(pl.multiple_of(s * LANES, LANES), LANES)
                 for hi in range(2):
                     mis[t, hi, :, at] = cor[t, hi]
-                mate_in = remote(cor.at[t], cols(s), dev_mate, cols(s_mate))
                 for k in (1, 2, 3):
                     far = lax.rem(z + 4 - k, 4) * 2 + xl
                     gathered[t].append((remote(cor.at[t], cols(s), dev_z[k], cols(far))))
@@ -246,11 +247,6 @@
             yield
             backward(mine)
             yield
-            if c == chunks - 1:
-                mate_in.wait_recv()
-                for k in (1, 2, 3):
-                    far = lax.rem(z + 4 - k, 4) * 2 + 1 - xl
-                    gathered[t].append((remote(cols(s_mate), cols(s_mate), dev_z[k], cols(far))))
             core_in.wait_recv()
 
             def add(block, *others):
@@ -291,6 +287,8 @@
                 add(block, theirs_of(block), *[ry0.at[t, c, k, at, rr] for k in range(3)])
                 if far:
                     last_x.append(remote(bk.at[t, c, mine + block, rr], rx0.at[t, c, rr], dev_x))
+            if c == chunks - 1:
+                mate_in = remote(cor.at[t], cols(s), dev_mate, cols(s_mate))
             yield
             x_new = x1 if t == 0 else xo
 
@@ -321,6 +319,11 @@
                 cp.wait_recv()
             renew(y * 2 + xh, 0, rx0.at[t, c, rr])
             ins_x = [send(span(y * 2 + xh, 1), dev_x, span(y * 2 + 1 - xh, 1))]
+            if c == chunks - 1:
+                mate_in.wait_recv()
+                for k in (1, 2, 3):
+                    far = lax.rem(z + 4 - k, 4) * 2 + 1 - xl
+                    gathered[t].append((remote(cols(s_mate), cols(s_mate), dev_z[k], cols(far))))
             yield
             for cp in ins_y:
                 cp.wait_recv()
@@ -358,10 +361,6 @@
         lay_out(theirs + 8)
         core_in[2].wait_recv()
         lay_out(theirs)
-        done = pltpu.make_async_copy(obuf.at[at_rows, :], upd_hbm.at[at_rows, :],
-                                     local_sem.at[steps + chunks + 2 + subsets + c])
-        done.start()
-        out_copies.append(done)
 
     live = [chain(c) for c in range(chunks)]
     for c in ORDER:
@@ -369,9 +368,6 @@
     for t in range(subsets):
         for cp in gathered[t]:
             cp.wait_recv()
-        cp = pltpu.make_async_copy(mis.at[t], mis_hbm.at[t], local_sem.at[steps + chunks + 2 + t])
-        cp.start()
-        out_copies.append(cp)
     for cp in out_copies:
         cp.wait()
     for cp in pending:
@@ -389,14 +385,14 @@
     vb = voxels // LANES
     f32 = jnp.float32
     copies = 34 * subsets * chunks + 7 * subsets
-    any_spec = pl.BlockSpec(memory_space=pl.ANY)
+    hbm = pl.BlockSpec(memory_space=pltpu.HBM)
     smem = pl.BlockSpec(memory_space=pltpu.SMEM)
     upd, mis = pl.pallas_call(
         lambda *refs: kernel(chunks, *refs),
-        out_shape=(jax.ShapeDtypeStruct((slices, voxels), f32),
-                   jax.ShapeDtypeStruct((subsets, 2, slices, band), f32)),
-        in_specs=[smem, smem, any_spec, any_spec, any_spec],
-        out_specs=(any_spec, any_spec),
+        out_shape=(pltpu.VMEM((slices, voxels), f32),
+                   pltpu.VMEM((subsets, 2, slices, band), f32)),
+        in_specs=[smem, smem, hbm, hbm, hbm],
+        out_specs=(pl.BlockSpec(memory_space=pltpu.VMEM), pl.BlockSpec(memory_space=pltpu.VMEM)),
         scratch_shapes=[
             pltpu.VMEM((subsets, voxels, band), jnp.bfloat16),
             pltpu.VMEM((slices, voxels), f32),
@@ -418,8 +414,6 @@
             pltpu.VMEM((subsets, chunks, r, LANES), f32),
             pltpu.VMEM((subsets, chunks, 3, r, LANES), f32),
             pltpu.VMEM((subsets, chunks, 4, r, LANES), f32),
-            pltpu.VMEM((slices, voxels), f32),
-            pltpu.VMEM((subsets, 2, slices, band), f32),
             pltpu.SemaphoreType.DMA((voxels // KB + chunks * 2 + 2 + subsets,)),
             pltpu.SemaphoreType.DMA((copies,)),
             pltpu.SemaphoreType.DMA((copies,)),
@@ -431,24 +425,20 @@
     return place(order, upd, mis)
 
 
-def place_kernel(order_ref, upd_hbm, mis_hbm, out_upd, out_mis, upd, mis, sem):
+def place_kernel(order_ref, upd, mis, out_upd, out_mis, sem):
     band = mis.shape[3]
     rows = upd.shape[0] // 4
-    moves = []
+    stores = []
     for t in range(mis.shape[0]):
         view = order_ref[t]
         for hi in range(2):
-            moves.append((mis_hbm.at[t, hi], mis.at[t, hi], out_mis.at[view, :, pl.ds(hi * band, band)]))
+            stores.append(pltpu.make_async_copy(
+                mis.at[t, hi], out_mis.at[view, :, pl.ds(hi * band, band)], sem.at[len(stores)]))
     for i in range(4):
         at = pl.ds(i * rows, rows)
-        moves.append((upd_hbm.at[at, :], upd.at[at, :], out_upd.at[at, :]))
-    loads = [pltpu.make_async_copy(a, b, sem.at[0, i]) for i, (a, b, _) in enumerate(moves)]
-    stores = [pltpu.make_async_copy(b, c, sem.at[1, i]) for i, (_, b, c) in enumerate(moves)]
-    for cp in loads:
+        stores.append(pltpu.make_async_copy(upd.at[at, :], out_upd.at[at, :], sem.at[len(stores)]))
+    for cp in stores:
         cp.start()
-    for load, store in zip(loads, stores):
-        load.wait()
-        store.start()
     for cp in stores:
         cp.wait()
 
@@ -460,12 +450,13 @@
         place_kernel,
         out_shape=(jax.ShapeDtypeStruct(upd.shape, upd.dtype),
                    jax.ShapeDtypeStruct((subsets, slices, 2 * band), mis.dtype)),
-        in_specs=[pl.BlockSpec(memory_space=pltpu.SMEM), any_spec, any_spec],
+        in_specs=[pl.BlockSpec(memory_space=pltpu.SMEM), pl.BlockSpec(memory_space=pltpu.VMEM), pl.BlockSpec(memory_space=pltpu.VMEM)],
         out_specs=(any_spec, any_spec),
-        scratch_shapes=[pltpu.VMEM(upd.shape, upd.dtype), pltpu.VMEM(mis.shape, mis.dtype),
-                        pltpu.SemaphoreType.DMA((2, 8))],
+        scratch_shapes=[pltpu.SemaphoreType.DMA((8,))],
+        compiler_params=pltpu.CompilerParams(vmem_limit_bytes=2**20),
         name="place",
-    )(order, upd, mis)
+    )(order, pltpu.with_memory_space_constraint(upd, pltpu.VMEM),
+      pltpu.with_memory_space_constraint(mis, pltpu.VMEM))
 
 
 def solution(mesh):

time: 105 us -> 101 us (0.962)
  Pallas kernels: 105 us -> 99.9 us
    pallas_call x1, Pallas kernels: 100 us -> 97.3 us  [per_device(): pl.pallas_call(lambda *refs: kernel(chunks, *refs), out_shape=(pltpu.VMEM...]
    pallas_call x1, Pallas kernels: 4.24 us -> 2.61 us  [place(): pl.pallas_call(place_kernel, out_shape=(jax.ShapeDtypeStruct(upd.shape, u...]
where the time goes in v4:
time: 101 us
  Pallas kernels  99.9 us (99%)
    pallas_call x1, Pallas kernels, per_device(): pl.pallas_call(lambda *refs: kernel(chunks, *refs), out_shape=(pltpu.VMEM...  97.3 us
    pallas_call x1, Pallas kernels, place(): pl.pallas_call(place_kernel, out_shape=(jax.ShapeDtypeStruct(upd.shape, u...  2.61 us

profile of v4, /device:TPU:1, one launch (start us, length us, event | category | flops | bytes accessed | tf_op | source)
XLA Modules:
  0.0 100.6 jit_solution(10776941667619343903)
XLA Ops:
  0.6 0.0 copy-start
  0.6 97.3 %sart.1 = (f32[128,4096]{1,0:T(8,128)S(1)}, f32[2,2,128,1024]{3,2,1,0:T(8,128)S(1)}) custom-call(s32[2]{0:T(128)} %order_ref.1, s32[2]{0:T(128)} %bitcast.1, f32[128,4096]{1,0:T(8,128)} %refs_2_.1, bf16[2,128,2048]{2,1,0:T(8,128)(2,1)} %refs_3_.1, bf16[2,4096,1024]{2,1,0:T(8,128)(2,1)} %refs_4_.1), custom_call_target="tpu_custom_call" | custom-call | tf_op jit(solution)/shard_map/sart/pallas_call | solution.py:390
  98.0 0.0 copy-done
  98.0 2.6 %place.1 = (f32[128,4096]{1,0:T(8,128)}, f32[2,128,2048]{2,1,0:T(8,128)}) custom-call(s32[2]{0:T(128)S(1)} %copy-done, f32[128,4096]{1,0:T(8,128)S(1)} %get-tuple-element.4.upd, f32[2,2,128,1024]{3,2,1,0:T(8,128)S(1)} %get-tuple-element.5.mis), custom_call_target="tpu_custom_call" | custom-call | tf_op jit(solution)/shard_map/place/pallas_call | solution.py:449
Async XLA Ops:
  0.6 97.3 %copy-start = (s32[2]{0:T(128)S(1)}, s32[2]{0:T(128)}, u32[]{:S(2)}) copy-start(s32[2]{0:T(128)} %order_ref.1) | copy-start | bytes 28

commit v5 on v4

--- a/solution.py
+++ b/solution.py
@@ -156,8 +156,6 @@
                 lax.fori_loop(2, 3, joined, 0)
                 core_in[2].wait_recv()
                 lax.fori_loop(3, 4, joined, 0)
-            if t == 0 and c == 0:
-                pl.semaphore_wait(barrier, 12)
             folded = pltpu.roll(acc[c, rr, :], shift, 1)
             if ext:
                 tail = folded[rows:, :]
@@ -167,6 +165,8 @@
                 fs[t, c, b, only, :] = folded[:rows, b * LANES:(b + 1) * LANES]
                 if ext:
                     fs[t, c, b, pl.ds(rows, ext), :] = tail[:, b * LANES:(b + 1) * LANES]
+            if t == 0 and c == 0:
+                pl.semaphore_wait(barrier, 12)
             arrivals = []
             for k, (dz, dx) in enumerate(SLAB_PEERS, 1):
                 peer = across(dz, dx)
@@ -238,7 +238,7 @@
                     for j in range(KB // LANES):
                         bk[t, c, vb + j, rr, :] = res[:r, j * LANES:(j + 1) * LANES]
                     return carry
-                lax.fori_loop(0, half * LANES // KB, step, 0)
+                lax.fori_loop(0, half * LANES // KB, step, 0, unroll=True)
 
             theirs = (1 - core) * half
             mine = core * half
@@ -363,14 +363,23 @@
         lay_out(theirs)
 
     live = [chain(c) for c in range(chunks)]
-    for c in ORDER:
+    marks, drained = [], 0
+    for at, c in enumerate(ORDER):
         next(live[c], None)
+        marks.append(len(pending))
+        if at >= 4 and at < len(ORDER) - 2:
+            for cp in pending[drained:marks[at - 4]]:
+                cp.wait_send()
+            drained = max(drained, marks[at - 4])
+        if at == len(ORDER) * 3 // 4:
+            for cp in gathered[0]:
+                cp.wait_recv()
     for t in range(subsets):
-        for cp in gathered[t]:
+        for cp in gathered[t] if t else ():
             cp.wait_recv()
     for cp in out_copies:
         cp.wait()
-    for cp in pending:
+    for cp in pending[drained:]:
         cp.wait_send()
 
 

time: 101 us -> 100 us (0.990)
  no operation moved by 1% of the time
where the time goes in v5:
time: 100 us; the launch traced here: 99.9 us
  Pallas kernels  99.2 us (99%)
    pallas_call x1, Pallas kernels, per_device(): pl.pallas_call(lambda *refs: kernel(chunks, *refs), out_shape=(pltpu.VMEM...  96.6 us
    pallas_call x1, Pallas kernels, place(): pl.pallas_call(place_kernel, out_shape=(jax.ShapeDtypeStruct(upd.shape, u...  2.61 us

profile of v5, /device:TPU:1, one launch (start us, length us, event | category | flops | bytes accessed | tf_op | source)
XLA Modules:
  0.0 99.9 jit_solution(6210700758177463229)
XLA Ops:
  0.6 0.0 copy-start
  0.6 96.6 %sart.1 = (f32[128,4096]{1,0:T(8,128)S(1)}, f32[2,2,128,1024]{3,2,1,0:T(8,128)S(1)}) custom-call(s32[2]{0:T(128)} %order_ref.1, s32[2]{0:T(128)} %bitcast.1, f32[128,4096]{1,0:T(8,128)} %refs_2_.1, bf16[2,128,2048]{2,1,0:T(8,128)(2,1)} %refs_3_.1, bf16[2,4096,1024]{2,1,0:T(8,128)(2,1)} %refs_4_.1), custom_call_target="tpu_custom_call" | custom-call | tf_op jit(solution)/shard_map/sart/pallas_call | solution.py:399
  97.3 0.0 copy-done
  97.3 2.6 %place.1 = (f32[128,4096]{1,0:T(8,128)}, f32[2,128,2048]{2,1,0:T(8,128)}) custom-call(s32[2]{0:T(128)S(1)} %copy-done, f32[128,4096]{1,0:T(8,128)S(1)} %get-tuple-element.4.upd, f32[2,2,128,1024]{3,2,1,0:T(8,128)S(1)} %get-tuple-element.5.mis), custom_call_target="tpu_custom_call" | custom-call | tf_op jit(solution)/shard_map/place/pallas_call | solution.py:458
Async XLA Ops:
  0.6 96.6 %copy-start = (s32[2]{0:T(128)S(1)}, s32[2]{0:T(128)}, u32[]{:S(2)}) copy-start(s32[2]{0:T(128)} %order_ref.1) | copy-start | bytes 28

commit v6 on v5

--- a/solution.py
+++ b/solution.py
@@ -213,6 +213,27 @@
             yield
             for cp in arrivals:
                 cp.wait_recv()
+            g = jnp.concatenate([gr[t, c, b] for b in range(nb)], axis=1)
+            g = pltpu.roll(g, jnp.where(shift == 0, 0, band - shift), 1).astype(jnp.bfloat16)
+            bandb[c, only, :] = g
+            if ext:
+                bandb[c, pl.ds(rows, 2 * ext), :] = jnp.ones((2 * ext, band), jnp.bfloat16)
+
+            def backward(base):
+                def step(n, carry):
+                    vb = base + n * (KB // LANES)
+                    wk = wv[view_t, pl.ds(pl.multiple_of(vb * LANES, LANES), KB), :]
+                    res = lax.dot_general(bandb[c, pl.ds(0, m), :], wk, (((1,), (1,)), ((), ())),
+                                          preferred_element_type=jnp.float32)
+                    for j in range(KB // LANES):
+                        bk[t, c, vb + j, rr, :] = res[:r, j * LANES:(j + 1) * LANES]
+                    return carry
+                lax.fori_loop(0, half * LANES // KB, step, 0, unroll=True)
+
+            theirs = (1 - core) * half
+            mine = core * half
+            backward(theirs)
+            core_in = remote(bk.at[t, c, pl.ds(theirs, half), rr], rc.at[t, c, :, rr], dev_core)
             if c == chunks - 1:
                 def cols(slab):
                     at = pl.ds(pl.multiple_of(slab * LANES, LANES), LANES)
@@ -223,27 +244,6 @@
                 for k in (1, 2, 3):
                     far = lax.rem(z + 4 - k, 4) * 2 + xl
                     gathered[t].append((remote(cor.at[t], cols(s), dev_z[k], cols(far))))
-            g = jnp.concatenate([gr[t, c, b] for b in range(nb)], axis=1)
-            g = pltpu.roll(g, jnp.where(shift == 0, 0, band - shift), 1).astype(jnp.bfloat16)
-            bandb[c, only, :] = g
-            if ext:
-                bandb[c, pl.ds(rows, 2 * ext), :] = jnp.ones((2 * ext, band), jnp.bfloat16)
-
-            def backward(base):
-                def step(n, carry):
-                    vb = base + n * (KB // LANES)
-                    wk = wv[view_t, pl.ds(pl.multiple_of(vb * LANES, LANES), KB), :]
-                    res = lax.dot_general(bandb[c, pl.ds(0, m), :], wk, (((1,), (1,)), ((), ())),
-                                          preferred_element_type=jnp.float32)
-                    for j in range(KB // LANES):
-                        bk[t, c, vb + j, rr, :] = res[:r, j * LANES:(j + 1) * LANES]
-                    return carry
-                lax.fori_loop(0, half * LANES // KB, step, 0, unroll=True)
-
-            theirs = (1 - core) * half
-            mine = core * half
-            backward(theirs)
-            core_in = remote(bk.at[t, c, pl.ds(theirs, half), rr], rc.at[t, c, :, rr], dev_core)
             yield
             backward(mine)
             yield
@@ -261,15 +261,15 @@
             other_x = 8 + (1 - xh) * 4
             own_x = 8 + xh * 4
             ins_y, ins_x = [], []
-            for j in range(4):
-                add(other_x + j, theirs_of(other_x + j))
-            ins_x.append(remote(bk.at[t, c, pl.ds(mine + other_x, 4), rr], rx1.at[t, c, :, rr], dev_x))
             for k in (2, 1, 3):
                 block = turned(k) * 2
                 for j in range(2):
                     add(block + j, theirs_of(block + j))
                 ins_y.append(remote(bk.at[t, c, pl.ds(mine + block, 2), rr],
                                     ry0.at[t, c, k - 1, :, rr], dev_y(k)))
+            for j in range(4):
+                add(other_x + j, theirs_of(other_x + j))
+            ins_x.append(remote(bk.at[t, c, pl.ds(mine + other_x, 4), rr], rx1.at[t, c, :, rr], dev_x))
             yield
             for cp in ins_x:
                 cp.wait_recv()

time: 100 us -> 99.6 us (level)
  no operation moved by 1% of the time
where the time goes in v6:
time: 99.6 us; the launch traced here: 99.5 us
  Pallas kernels  98.8 us (99%)
    pallas_call x1, Pallas kernels, per_device(): pl.pallas_call(lambda *refs: kernel(chunks, *refs), out_shape=(pltpu.VMEM...  96.2 us
    pallas_call x1, Pallas kernels, place(): pl.pallas_call(place_kernel, out_shape=(jax.ShapeDtypeStruct(upd.shape, u...  2.61 us

profile of v6, /device:TPU:1, one launch (start us, length us, event | category | flops | bytes accessed | tf_op | source)
XLA Modules:
  0.0 99.5 jit_solution(2756540469293226082)
XLA Ops:
  0.6 0.0 copy-start
  0.6 96.2 %sart.1 = (f32[128,4096]{1,0:T(8,128)S(1)}, f32[2,2,128,1024]{3,2,1,0:T(8,128)S(1)}) custom-call(s32[2]{0:T(128)} %order_ref.1, s32[2]{0:T(128)} %bitcast.1, f32[128,4096]{1,0:T(8,128)} %refs_2_.1, bf16[2,128,2048]{2,1,0:T(8,128)(2,1)} %refs_3_.1, bf16[2,4096,1024]{2,1,0:T(8,128)(2,1)} %refs_4_.1), custom_call_target="tpu_custom_call" | custom-call | tf_op jit(solution)/shard_map/sart/pallas_call | solution.py:399
  96.8 0.0 copy-done
  96.8 2.6 %place.1 = (f32[128,4096]{1,0:T(8,128)}, f32[2,128,2048]{2,1,0:T(8,128)}) custom-call(s32[2]{0:T(128)S(1)} %copy-done, f32[128,4096]{1,0:T(8,128)S(1)} %get-tuple-element.4.upd, f32[2,2,128,1024]{3,2,1,0:T(8,128)S(1)} %get-tuple-element.5.mis), custom_call_target="tpu_custom_call" | custom-call | tf_op jit(solution)/shard_map/place/pallas_call | solution.py:458
Async XLA Ops:
  0.6 96.2 %copy-start = (s32[2]{0:T(128)S(1)}, s32[2]{0:T(128)}, u32[]{:S(2)}) copy-start(s32[2]{0:T(128)} %order_ref.1) | copy-start | bytes 28
